TPU v7x, 256 devices: a whole 4x4x8 slice. The times are simulated.
256 devices in a mesh: grid: 8 (over y, core), wide: 32 (over z, x).
Axes of the slice: x: 4, y: 4, z: 8, core: 2. Of those that a mesh axis runs over, the one named last changes fastest.
Arguments:
- values: bfloat16 [3584, 64, 4096], P(('grid', 'wide')), may hold values from 0 to 1
- a_block: int32 [3584], P(('grid', 'wide')), may hold values from 0 to 63, as said below
- b_block: int32 [3584], P(('grid', 'wide')), may hold values from 0 to 15
- c_block: int32 [3584], P(('grid', 'wide')), may hold values from 0 to 63
- held: int32 [3584], P(('grid', 'wide')), may hold values from 0 to 1, as said below
- factor_a: bfloat16 [32768, 256], P(('grid', 'wide')), may hold values from -6 to 6
- factor_b: bfloat16 [32768, 256], P(('wide', 'grid')), may hold values from -2.390625 to 2.390625
- factor_c: bfloat16 [4096, 256], replicated, may hold values from -2.390625 to 2.390625
Outputs:
- next_a: float32 [32768, 256], P(('grid', 'wide'))
- next_b: float32 [32768, 256], P(('wide', 'grid'))
- held_loss: float32 [], replicated
Inputs may be any that keep to these rules, and one draw needn't show every extreme that they name: Among the blocks of one device, at most 1 have a_block values with the same a_block // 2; on some device some such value is shared by exactly 1 block. Every device holds 1 to 3 held-out blocks; some device holds exactly 3.
All inputs are finite; a program needn't handle non-finite values.
Results may differ from a plain program's by a relative error of at most 0.0011.
Values may be sent and summed in bfloat16 or wider, within the bound.
No kernel may reach another device: no remote copies, remote signals or barrier semaphores. Data moves between devices by JAX's collectives and lax.ppermute only.
A program may use at most 64 MiB of HBM per device.

v0:
```python
import jax
import jax.numpy as jnp
from jax import lax
from jax.sharding import PartitionSpec as P

step_size = 0.05


def block_terms(inputs):
    entries, a_rows, b_rows, c_rows, flag = inputs
    side = a_rows.shape[0]
    width = a_rows.shape[1]
    khatri = (
        b_rows.astype(jnp.float32)[:, None, :] * c_rows.astype(jnp.float32)[None, :, :]
    ).astype(jnp.bfloat16)
    khatri = khatri.reshape(side * side, width)
    model = lax.dot_general(
        a_rows, khatri, (((1,), (1,)), ((), ())), preferred_element_type=jnp.float32
    )
    entry_f = entries.astype(jnp.float32)
    resid = ((jax.nn.sigmoid(model) - entry_f) * (1.0 - flag)).astype(jnp.bfloat16)
    loss_part = jnp.sum(jax.nn.softplus(model) - entry_f * model) * flag
    grad_rows = jnp.dot(resid, khatri, preferred_element_type=jnp.float32)
    partial_sum = lax.dot_general(
        resid, a_rows, (((0,), (0,)), ((), ())), preferred_element_type=jnp.float32
    )
    grad_cols = jnp.sum(
        partial_sum.reshape(side, side, width) * c_rows.astype(jnp.float32)[None, :, :], axis=1
    )
    return (grad_rows, grad_cols, loss_part)


def per_device(values, a_block, b_block, c_block, held, factor_a, factor_b, factor_c):
    blocks = values.shape[0]
    side = values.shape[1]
    width = factor_a.shape[1]
    highest = lax.Precision.HIGHEST
    own_blocks = factor_a.shape[0] // side
    wide_count = lax.axis_size("wide")
    b_panel = lax.all_gather(factor_b, "grid", axis=0, tiled=True)
    b_rows = b_panel.reshape(-1, side, width)[b_block]
    c_rows = factor_c.reshape(-1, side, width)[c_block]
    a_panel = lax.all_gather(factor_a, "wide", axis=0, tiled=True)
    a_rows = a_panel.reshape(-1, side, width)[a_block]
    flags = held.astype(jnp.float32)
    grad_rows, grad_cols, loss_parts = lax.map(block_terms, (values, a_rows, b_rows, c_rows, flags))
    panel_blocks = own_blocks * wide_count
    matches = (a_block[:, None] == jnp.arange(panel_blocks)[None, :]).astype(jnp.float32)
    panel_grad = jnp.einsum("np,nk->pk", matches, grad_rows.reshape(blocks, -1), precision=highest)
    grad_a = lax.psum_scatter(
        panel_grad.reshape(panel_blocks * side, width), "wide", scatter_dimension=0, tiled=True
    )
    b_panel_blocks = b_panel.shape[0] // side
    b_matches = (b_block[:, None] == jnp.arange(b_panel_blocks)[None, :]).astype(jnp.float32)
    b_panel_grad = jnp.einsum(
        "np,nk->pk", b_matches, grad_cols.reshape(blocks, -1), precision=highest
    )
    grad_b = lax.psum_scatter(
        b_panel_grad.reshape(b_panel_blocks * side, width), "grid", scatter_dimension=0, tiled=True
    )
    loss_total, held_total = lax.psum((jnp.sum(loss_parts), jnp.sum(flags)), ("grid", "wide"))
    held_loss = loss_total / (held_total * (side * side * side))
    next_a = factor_a.astype(jnp.float32) - step_size * grad_a
    next_b = factor_b.astype(jnp.float32) - step_size * grad_b
    return (next_a, next_b, held_loss)


def solution(mesh):
    in_specs = (
        P(("grid", "wide"), None, None),
        P(("grid", "wide")),
        P(("grid", "wide")),
        P(("grid", "wide")),
        P(("grid", "wide")),
        P(("grid", "wide"), None),
        P(("wide", "grid"), None),
        P(),
    )
    out_specs = (P(("grid", "wide"), None), P(("wide", "grid"), None), P())
    return jax.shard_map(
        per_device, mesh=mesh, in_specs=in_specs, out_specs=out_specs, check_vma=False
    )
```

profile of v0, /device:TPU:8, one launch (start us, length us, event | category | flops | bytes accessed | tf_op | source)
XLA Modules:
  0.0 559.0 jit_solution(8834478500784365606)
XLA Ops:
  10.6 13.5 %all_gather.7 = bf16[1024,256]{1,0:T(8,128)(2,1)S(1)} all-gather(bf16[128,256]{1,0:T(8,128)(2,1)} %param.16), channel_id=1, replica_groups=mesh['grid'=8,'wide'=32] {'grid'}, dimensions={0}, use_global_device_ids=true | all-gather | bytes 589824 | tf_op jit(solution)/shard_map/all_gather | solution.py:40
  25.5 66.0 %all-gather.2.cloned.1.call-done = bf16[4096,256]{1,0:T(8,128)(2,1)} async-done(((bf16[128,256]{1,0:T(8,128)(2,1)}), bf16[4096,256]{1,0:T(8,128)(2,1)}) %all-gather.2.cloned.1.call-update) | async-done | bytes 2097168 | tf_op jit(solution)/shard_map/all_gather | solution.py:43
  91.5 2.9 gather_fusion
  94.4 195.9 %while.14 = (s32[]{:T(128)}, f32[14,64,256]{2,1,0:T(8,128)}, f32[14,64,256]{2,1,0:T(8,128)}, f32[14]{0:T(128)S(1)}, bf16[14,64,256]{2,1,0:T(8,128)(2,1)}, /*inde...) while((s32[]{:T(128)}, f32[14,64,256]{2,1,0:T(8,128)}, ...), condition=%wide.region_3.4_spmd, body=%wide.region_0.3_spmd.sunk | while | flops 411058176 | bytes 19072724 | solution.py:46
  97.1 3.3 fusion.34
  101.7 2.7 fusion.35
  111.1 3.3 fusion.34
  125.1 3.3 fusion.34
  139.1 3.3 fusion.34
  143.7 2.7 fusion.35
  153.1 3.3 fusion.34
  157.7 2.7 fusion.35
  167.1 3.3 fusion.34
  171.7 2.7 fusion.35
  181.1 3.3 fusion.34
  185.7 2.7 fusion.35
  195.1 3.3 fusion.34
  199.7 2.7 fusion.35
  209.0 3.3 fusion.34
  223.0 3.3 fusion.34
  227.6 2.7 fusion.35
  237.0 3.3 fusion.34
  251.0 3.3 fusion.34
  255.6 2.7 fusion.35
  265.0 3.3 fusion.34
  269.6 2.7 fusion.35
  279.0 3.3 fusion.34
  283.6 2.7 fusion.35
  296.1 3.9 fusion.12
  300.0 4.9 reshape.59
  306.8 73.6 %all-reduce = (f32[]{:T(128)}, f32[]{:T(128)}) all-reduce(f32[]{:T(128)} %reduce_sum.36, f32[]{:T(128)} %convert_reduce_fusion), channel_id=1, replica_groups=mesh['grid'=8,'wide'=32] {'grid','wide'}, use_global_device_ids=true, to_apply=%region_7.8 | all-reduce | flops 2 | bytes 16 | tf_op jit(solution)/shard_map/psum | solution.py:61
  383.3 166.5 %reduce-scatter.3.cloned.1.call-done = f32[128,256]{1,0:T(8,128)} async-done(((f32[4096,256]{1,0:T(8,128)}), f32[128,256]{1,0:T(8,128)}) %reduce-scatter.3.cloned.1.call-update) | async-done | bytes 131088 | tf_op jit(solution)/shard_map/reduce_scatter | solution.py:50
  (171 shorter events, 110.6 us)
Async XLA Ops:
  7.2 2.2 copy-start
  7.2 18.3 %copy-start.5 = (s32[14]{0:T(128)S(1)}, s32[14]{0:T(128)}, u32[]{:S(2)}) copy-start(s32[14]{0:T(128)} %param.11) | copy-start | bytes 172
  7.2 84.3 %all-gather.2.cloned.1.call-start = ((), (), s32[]{:S(2)}) async-start(), calls=%async_computation.2 | async-start | bytes 2162688 | tf_op jit(solution)/shard_map/all_gather | solution.py:43
  7.9 373.8 %reduce-scatter.5.cloned.1.call-start = ((), (), s32[]{:S(2)}) async-start(), calls=%async_computation.4 | async-start | bytes 1179648 | tf_op jit(solution)/shard_map/reduce_scatter | solution.py:58
  97.1 3.3 copy-start.1
  111.1 3.3 copy-start.1
  125.1 3.3 copy-start.1
  139.1 3.3 copy-start.1
  153.1 3.3 copy-start.1
  167.1 3.3 copy-start.1
  181.1 3.3 copy-start.1
  195.0 3.3 copy-start.1
  209.0 3.3 copy-start.1
  223.0 3.3 copy-start.1
  237.0 3.3 copy-start.1
  251.0 3.3 copy-start.1
  265.0 3.3 copy-start.1
  279.0 3.3 copy-start.1
  290.3 1.9 copy-start.4
  294.2 255.6 %reduce-scatter.3.cloned.1.call-start = ((), (), s32[]{:S(2)}) async-start(), calls=%async_computation.3 | async-start | bytes 4325376 | tf_op jit(solution)/shard_map/reduce_scatter | solution.py:50
  304.9 0.7 copy-start.6
  304.9 76.8 %copy-start.2 = (bf16[128,256]{1,0:T(8,128)(2,1)S(1)}, bf16[128,256]{1,0:T(8,128)(2,1)}, u32[]{:S(2)}) copy-start(bf16[128,256]{1,0:T(8,128)(2,1)} %param.16) | copy-start | bytes 196612
  304.9 244.9 %copy-start.3 = (bf16[128,256]{1,0:T(8,128)(2,1)S(1)}, bf16[128,256]{1,0:T(8,128)(2,1)}, u32[]{:S(2)}) copy-start(bf16[128,256]{1,0:T(8,128)(2,1)} %param.15) | copy-start | bytes 196612
Sparse Core Ops, SparseCore 0:
  10.6 80.8 all-gather.1
  294.3 28.5 reduce-scatter.4
  326.8 222.9 reduce-scatter.2
where the time goes:
time: 562 us; the launch traced here: 559 us
  waiting for transfers between devices  233 us (41%)
  matrix products  115 us (20%)
  blocking collectives  87.2 us (16%)
  local copies, waits for them, and re-layouts  52.6 us (9%)
  loops' own time  27.7 us (5%)
  other arithmetic  26.8 us (5%)
  between operations  16.3 us (3%)
    reduce_scatter x1, waiting for transfers between devices, per_device(): lax.psum_scatter(panel_grad.reshape(panel_blocks * side, width), 'wide',...  166 us
    psum x1, blocking collectives, per_device(): lax.psum((jnp.sum(loss_parts), jnp.sum(flags)), ('grid', 'wide'))  73.6 us
    all_gather x1, waiting for transfers between devices, per_device(): a_panel = lax.all_gather(factor_a, 'wide', axis=0, tiled=True)  66 us
    dot_general x14, matrix products, block_terms(): lax.dot_general(a_rows, khatri, (((1,), (1,)), ((), ())), preferred_eleme...  46.2 us
    dot_general x14, matrix products, block_terms(): grad_rows = jnp.dot(resid, khatri, preferred_element_type=jnp.float32)  37.5 us
    another operation x1, loops' own time, per_device(): lax.map(block_terms, (values, a_rows, b_rows, c_rows, flags))  27.7 us
    dot_general x14, matrix products, block_terms(): lax.dot_general(resid, a_rows, (((0,), (0,)), ((), ())), preferred_elemen...  26.9 us
    dot_general x14, local copies, waits for them, and re-layouts, block_terms(): lax.dot_general(resid, a_rows, (((0,), (0,)), ((), ())), preferred_elemen...  18.7 us
  transfers between devices with their start and end apart: 3, of which 2 were waited for; matrix products, arithmetic and copies ran while one was open for 3% of the time, Pallas kernels for 0%

commit v1 on v0

v1 whole, which is shorter than its diff:
```python
import jax
import jax.numpy as jnp
from jax import lax
from jax.experimental import pallas as pl
from jax.experimental.pallas import tpu as pltpu
from jax.sharding import Mesh, PartitionSpec as P

step_size = 0.05
f32 = jnp.float32
bf16 = jnp.bfloat16
GROUP = 8


def block_kernel(
    tab, values_ref, a_ref, b_ref, c_ref, slots_ref, b_grad_ref, loss_ref
):
    i = pl.program_id(0)

    @pl.when(i == 0)
    def _():
        slots_ref[...] = jnp.zeros_like(slots_ref)
        b_grad_ref[...] = jnp.zeros_like(b_grad_ref)
        loss_ref[...] = jnp.zeros_like(loss_ref)

    a_rows = a_ref[0]
    c_rows = c_ref[0]
    side, width = a_rows.shape
    held = tab[3, i]
    span = GROUP * side

    def khatri_of(group):
        b_rows = b_ref[0, pl.ds(group * GROUP, GROUP), :]
        product = b_rows.astype(f32)[:, None, :] * c_rows.astype(f32)[None, :, :]
        return product.astype(bf16).reshape(span, width)

    def model_of(khatri):
        return lax.dot_general(
            a_rows, khatri, (((1,), (1,)), ((), ())), preferred_element_type=f32
        )

    @pl.when(held == 0)
    def _():
        c_f = c_rows.astype(f32)
        b_index = tab[1, i]
        slot = tab[4, i]
        grad_rows = jnp.zeros((side, width), f32)
        for group in range(side // GROUP):
            khatri = khatri_of(group)
            model = model_of(khatri)
            entries = values_ref[0, :, group * span : (group + 1) * span].astype(f32)
            sigmoid = 0.5 * jnp.tanh(0.5 * model) + 0.5
            resid = (sigmoid - entries).astype(bf16)
            grad_rows = grad_rows + jnp.dot(resid, khatri, preferred_element_type=f32)
            partial_sum = lax.dot_general(
                resid, a_rows, (((0,), (0,)), ((), ())), preferred_element_type=f32
            )
            cols = jnp.sum(partial_sum.reshape(GROUP, side, width) * c_f[None], axis=1)
            at = (b_index, pl.ds(group * GROUP, GROUP), slice(None))
            b_grad_ref[at] = b_grad_ref[at] + cols
        slots_ref[slot, pl.ds(0, side), :] = grad_rows
        slots_ref[slot, pl.ds(side, 8), :] = jnp.full((8, width), tab[5, i].astype(f32), f32)

    @pl.when(held != 0)
    def _():
        total = jnp.zeros((side, span), f32)
        for group in range(side // GROUP):
            model = model_of(khatri_of(group))
            entries = values_ref[0, :, group * span : (group + 1) * span].astype(f32)
            soft = jnp.maximum(model, 0.0) + jnp.log1p(jnp.exp(-jnp.abs(model)))
            total = total + (soft - entries * model)
        folded = total.reshape(side // 8, 8, span).sum(axis=0)
        lanes = folded[:, 0:128]
        for k in range(1, span // 128):
            lanes = lanes + folded[:, k * 128 : (k + 1) * 128]
        loss_ref[...] = loss_ref[...] + lanes


def run_blocks(table, values, a_panel, b_panel, c_panel, n_slots):
    side, width = a_panel.shape[1:]
    whole3 = lambda i, tab: (0, 0, 0)
    grid_spec = pltpu.PrefetchScalarGridSpec(
        num_scalar_prefetch=1,
        grid=(values.shape[0],),
        in_specs=[
            pl.BlockSpec((1,) + values.shape[1:], lambda i, tab: (i, 0, 0)),
            pl.BlockSpec((1, side, width), lambda i, tab: (tab[0, i], 0, 0)),
            pl.BlockSpec((1, side, width), lambda i, tab: (tab[1, i], 0, 0)),
            pl.BlockSpec((1, side, width), lambda i, tab: (tab[2, i], 0, 0)),
        ],
        out_specs=[
            pl.BlockSpec((n_slots, side + 8, width), whole3),
            pl.BlockSpec(b_panel.shape, whole3),
            pl.BlockSpec((8, 128), lambda i, tab: (0, 0)),
        ],
    )
    return pl.pallas_call(
        block_kernel,
        out_shape=[
            jax.ShapeDtypeStruct((n_slots, side + 8, width), f32),
            jax.ShapeDtypeStruct(b_panel.shape, f32),
            jax.ShapeDtypeStruct((8, 128), f32),
        ],
        grid_spec=grid_spec,
    )(table, values, a_panel, b_panel, c_panel)


def step(values, a_block, b_block, c_block, held, factor_a, factor_b, factor_c):
    side, width = values.shape[1], factor_a.shape[1]
    nz, nx = lax.axis_size("z"), lax.axis_size("x")
    grid_axes, wide_axes = ("y", "core"), ("z", "x")
    n_grid, n_wide = lax.axis_size(grid_axes), nz * nx
    z, x = lax.axis_index("z"), lax.axis_index("x")
    own = factor_a.shape[0] // side

    def shift(v, axis, by):
        n = lax.axis_size(axis)
        return lax.ppermute(v, axis, [(k, (k + by) % n) for k in range(n)])

    column = jnp.concatenate([factor_a] + [shift(factor_a, "z", s) for s in range(1, nz)])
    b_panel = lax.all_gather(factor_b, grid_axes, axis=0, tiled=True).reshape(-1, side, width)
    half = column.shape[0] // 2
    ahead = shift(column, "x", 1)
    back = shift(column, "x", nx - 1)
    far = [shift(ahead[:half], "x", 1), shift(back[half:], "x", nx - 1)]
    a_panel = jnp.concatenate([column, ahead, *far, back]).reshape(-1, side, width)
    c_panel = factor_c.reshape(-1, side, width)

    holder = a_block // own
    within = a_block % own
    s = (z - holder // nx) % nz
    q = (x - holder % nx) % nx
    table = jnp.stack([(q * nz + s) * own + within, b_block, c_block, held, holder, within])
    slots, b_grad, loss = run_blocks(table, values, a_panel, b_panel, c_panel, n_wide)

    totals = jnp.stack([jnp.sum(loss), jnp.sum(held).astype(f32)])
    extra = jnp.broadcast_to(totals[None, :, None], (n_grid, 2, width))
    extra = jnp.concatenate([extra, jnp.zeros((n_grid, 6, width), f32)], axis=1)
    sent = jnp.concatenate([b_grad.reshape(n_grid, -1, width), extra], axis=1)
    got = jnp.sum(lax.all_to_all(sent, grid_axes, 0, 0, tiled=True), axis=0)
    rows = factor_b.shape[0]
    grad_b = got[:rows]
    group_totals = jnp.broadcast_to(got[None, rows : rows + 2], (n_wide, 2, width))
    sent = lax.dynamic_update_slice(slots, group_totals, (0, side + 1, 0))
    got = lax.all_to_all(sent, wide_axes, 0, 0, tiled=True)
    which = got[:, side : side + 1, :1]
    grad_a = jnp.concatenate(
        [jnp.sum(jnp.where(which == k, got[:, :side], 0.0), axis=0) for k in range(own)]
    )
    totals = jnp.sum(got[:, side + 1 : side + 3, 0], axis=0)
    held_loss = totals[0] / (totals[1] * (side * side * side))
    next_a = factor_a.astype(f32) - step_size * grad_a
    next_b = factor_b.astype(f32) - step_size * grad_b
    return next_a, next_b, held_loss


def solution(mesh):
    fine = Mesh(mesh.devices.reshape(4, 2, 8, 4), ("y", "core", "z", "x"))
    blocks = ("y", "core", "z", "x")
    rows_b = ("z", "x", "y", "core")
    in_specs = (
        P(blocks, None, None), P(blocks), P(blocks), P(blocks), P(blocks),
        P(blocks, None), P(rows_b, None), P(),
    )
    out_specs = (P(blocks, None), P(rows_b, None), P())
    return jax.shard_map(step, mesh=fine, in_specs=in_specs, out_specs=out_specs, check_vma=False)
```

time: 562 us -> 193 us (0.34)
  waiting for transfers between devices: 233 us -> 60.4 us
  matrix products: 115 us -> 0 us
  blocking collectives: 87.2 us -> 35.8 us
  local copies, waits for them, and re-layouts: 52.6 us -> 12.8 us
  Pallas kernels: 0 us -> 38.6 us
  starting transfers between devices: 0.12 us -> 31.9 us
  loops' own time: 27.7 us -> 0 us
  other arithmetic: 26.8 us -> 7.89 us
  between operations: 16.3 us -> 3.88 us
    reduce_scatter x2 -> x0, waiting for transfers between devices: 166 us -> none  [the longest x1 166 us: per_device(): lax.psum_scatter(panel_grad.reshape(panel_blocks * side, width), 'wide',...]
    dot_general x44 -> x0, matrix products: 115 us -> none  [the longest x14 46.2 us: block_terms(): lax.dot_general(a_rows, khatri, (((1,), (1,)), ((), ())), preferred_eleme...]
    psum x1 -> x0, blocking collectives: 73.6 us -> none  [per_device(): lax.psum((jnp.sum(loss_parts), jnp.sum(flags)), ('grid', 'wide'))]
    all_gather x1 -> x0, waiting for transfers between devices: 66 us -> none  [per_device(): a_panel = lax.all_gather(factor_a, 'wide', axis=0, tiled=True)]
    all_to_all x0 -> x1, waiting for transfers between devices: none -> 54.9 us  [step(): got = lax.all_to_all(sent, wide_axes, 0, 0, tiled=True)]
    pallas_call x0 -> x1, Pallas kernels: none -> 38.6 us  [run_blocks(): pl.pallas_call(block_kernel, out_shape=[jax.ShapeDtypeStruct((n_slots, si...]
    another operation x1 -> x0, loops' own time: 27.7 us -> none  [per_device(): lax.map(block_terms, (values, a_rows, b_rows, c_rows, flags))]
    ppermute x0 -> x11, starting transfers between devices: none -> 24.9 us  [shift(): return lax.ppermute(v, axis, [(k, (k + by) % n) for k in range(n)])]
  transfers between devices with their start and end apart: 3 -> 12, of which waited for: 2 -> 5; matrix products, arithmetic and copies ran while one was open for 3% -> 5% of each run, Pallas kernels for 0% -> 0%
where the time goes in v1:
time: 193 us; the launch traced here: 191 us
  waiting for transfers between devices  60.4 us (31%)
  Pallas kernels  38.6 us (20%)
  blocking collectives  35.8 us (19%)
  starting transfers between devices  31.9 us (17%)
  local copies, waits for them, and re-layouts  12.8 us (7%)
  other arithmetic  7.89 us (4%)
  between operations  3.88 us (2%)
    all_to_all x1, waiting for transfers between devices, step(): got = lax.all_to_all(sent, wide_axes, 0, 0, tiled=True)  54.9 us
    pallas_call x1, Pallas kernels, run_blocks(): pl.pallas_call(block_kernel, out_shape=[jax.ShapeDtypeStruct((n_slots, si...  38.6 us
    ppermute x11, starting transfers between devices, shift(): return lax.ppermute(v, axis, [(k, (k + by) % n) for k in range(n)])  24.9 us
    all_to_all x1, blocking collectives, step(): got = jnp.sum(lax.all_to_all(sent, grid_axes, 0, 0, tiled=True), axis=0)  21.2 us
    all_gather x1, blocking collectives, step(): lax.all_gather(factor_b, grid_axes, axis=0, tiled=True)  14.6 us
    unnamed x24, local copies, waits for them, and re-layouts  7.65 us
    all_to_all x1, starting transfers between devices, step(): got = lax.all_to_all(sent, wide_axes, 0, 0, tiled=True)  6.99 us
    ppermute x11, waiting for transfers between devices, shift(): return lax.ppermute(v, axis, [(k, (k + by) % n) for k in range(n)])  5.43 us
  transfers between devices with their start and end apart: 12, of which 5 were waited for; matrix products, arithmetic and copies ran while one was open for 5% of the time, Pallas kernels for 0%

profile of v1, /device:TPU:8, one launch (start us, length us, event | category | flops | bytes accessed | tf_op | source)
XLA Modules:
  0.0 191.3 jit_solution(1283063645930697679)
XLA Ops:
  0.7 2.0 %collective-permute-start = (bf16[128,256]{1,0:T(8,128)(2,1)}, bf16[128,256]{1,0:T(8,128)(2,1)S(1)}, u32[]{:S(2)}, u32[]{:S(2)}) collective-permute-start(bf16[128,256]{1,0:T(8,128)(2,1)} %param.13), channel_id=1, source_target_pairs={{0,4},{4,8},{8,12},{12,16},{16,20},{20,24},{24,28},{28,0},{1,5},{5... | collective-permute-start | bytes 196616 | tf_op jit(solution)/shard_map/ppermute | solution.py:117
  2.7 3.3 %collective-permute-start.1 = (bf16[128,256]{1,0:T(8,128)(2,1)}, bf16[128,256]{1,0:T(8,128)(2,1)S(1)}, u32[]{:S(2)}, u32[]{:S(2)}) collective-permute-start(bf16[128,256]{1,0:T(8,128)(2,1)} %param.13), channel_id=1, source_target_pairs={{0,8},{4,12},{8,16},{12,20},{16,24},{20,28},{24,0},{28,4},{1,9},{5... | collective-permute-start | bytes 196616 | tf_op jit(solution)/shard_map/ppermute | solution.py:117
  5.9 4.0 %collective-permute-start.2 = (bf16[128,256]{1,0:T(8,128)(2,1)}, bf16[128,256]{1,0:T(8,128)(2,1)S(1)}, u32[]{:S(2)}, u32[]{:S(2)}) collective-permute-start(bf16[128,256]{1,0:T(8,128)(2,1)} %param.13), channel_id=1, source_target_pairs={{0,12},{4,16},{8,20},{12,24},{16,28},{20,0},{24,4},{28,8},{1,13},{... | collective-permute-start | bytes 196616 | tf_op jit(solution)/shard_map/ppermute | solution.py:117
  10.5 4.9 %collective-permute-start.4 = (bf16[128,256]{1,0:T(8,128)(2,1)}, bf16[128,256]{1,0:T(8,128)(2,1)S(1)}, u32[]{:S(2)}, u32[]{:S(2)}) collective-permute-start(bf16[128,256]{1,0:T(8,128)(2,1)} %param.13), channel_id=1, source_target_pairs={{0,20},{4,24},{8,28},{12,0},{16,4},{20,8},{24,12},{28,16},{1,21},{... | collective-permute-start | bytes 196616 | tf_op jit(solution)/shard_map/ppermute | solution.py:117
  15.5 1.5 constant_dynamic-update-slice_fusion.7
  17.0 2.7 %collective-permute-start.5 = (bf16[128,256]{1,0:T(8,128)(2,1)}, bf16[128,256]{1,0:T(8,128)(2,1)S(1)}, u32[]{:S(2)}, u32[]{:S(2)}) collective-permute-start(bf16[128,256]{1,0:T(8,128)(2,1)} %param.13), channel_id=1, source_target_pairs={{0,24},{4,28},{8,0},{12,4},{16,8},{20,12},{24,16},{28,20},{1,25},{... | collective-permute-start | bytes 196616 | tf_op jit(solution)/shard_map/ppermute | solution.py:117
  20.3 1.0 collective-permute-start.6
  21.3 0.6 constant_dynamic-update-slice_fusion.5
  22.6 0.6 constant_dynamic-update-slice_fusion.3
  23.8 0.9 collective-permute-done.5
  25.9 0.6 constant_dynamic-update-slice_fusion
  26.5 1.5 collective-permute-start.7
  28.0 1.7 collective-permute-start.9
  29.7 0.7 fusion.7
  30.4 14.6 %all_gather.3 = bf16[1024,256]{1,0:T(8,128)(2,1)} all-gather(bf16[128,256]{1,0:T(8,128)(2,1)} %param.14), channel_id=1, replica_groups=mesh['y'=4,'core'=2,'z'=8,'x'=4] {'y','core'}, dimensions={0}, use_global_device_ids=true | all-gather | bytes 589824 | tf_op jit(solution)/shard_map/all_gather | solution.py:120
  45.0 0.7 slice.37
  46.0 0.7 slice.38
  46.7 3.0 %collective-permute-start.10 = (bf16[512,256]{1,0:T(8,128)(2,1)}, bf16[512,256]{1,0:T(8,128)(2,1)}, u32[]{:S(2)}, u32[]{:S(2)}) collective-permute-start(bf16[512,256]{1,0:T(8,128)(2,1)} %slice.38), channel_id=1, source_target_pairs={{0,3},{1,0},{2,1},{3,2},{4,7},{5,4},{6,5},{7,6},{8,11},{9,8},{10,9... | collective-permute-start | bytes 786440 | tf_op jit(solution)/shard_map/ppermute | solution.py:117
  51.8 3.9 %collective-permute-done.8 = bf16[512,256]{1,0:T(8,128)(2,1)S(1)} collective-permute-done((bf16[512,256]{1,0:T(8,128)(2,1)}, bf16[512,256]{1,0:T(8,128)(2,1)S(1)}, u32[]{:S(2)}, u32[]{:S(2)}) %collective-permute-start.8) | collective-permute-done | bytes 262176 | tf_op jit(solution)/shard_map/ppermute | solution.py:117
  55.8 1.0 constant_dynamic-update-slice_fusion.9
  56.8 1.3 copy-done
  58.1 38.6 %shard_map.103 = (f32[32,72,256]{2,1,0:T(8,128)}, f32[16,64,256]{2,1,0:T(8,128)}, f32[8,128]{1,0:T(8,128)}) custom-call(s32[6,14]{1,0:T(8,128)} %stack.36.tab, bf16[14,64,4096]{2,1,0:T(8,128)(2,1)} %values_ref.1, bf16[64,64,256]{2,1,0:T(8,128)(2,1)} %bitcast.15, bf16[16,64,256]{2,1,0:T(8,128)(2,1)} %bitcast.16, bf16[64,64,256]{2,1,0:T(8,128)(2,1)} %bitcast.17), custom_call_target="tpu_custom_call" | custom-call | tf_op jit(solution)/shard_map/pallas_call | solution.py:96
  96.7 1.3 reduce_sum.54
  98.0 0.7 pad_maximum_fusion
  98.8 1.4 maximum_maximum_fusion
  100.2 21.2 %all_to_all.10 = f32[8,136,256]{2,1,0:T(8,128)S(1)} all-to-all(f32[8,136,256]{2,1,0:T(8,128)S(1)} %maximum_maximum_fusion), channel_id=1, replica_groups=mesh['y'=4,'core'=2,'z'=8,'x'=4] {'y','core'}, dimensions={0} | all-to-all | bytes 2228224 | tf_op jit(solution)/shard_map/all_to_all | solution.py:139
  121.4 1.8 dynamic_update_slice.3
  123.2 7.0 %all-to-all-start.1 = ((f32[32,72,256]{2,1,0:T(8,128)}), f32[32,72,256]{2,1,0:T(8,128)S(1)}, u32[]{:S(2)}, u32[]{:S(2)}) async-start(f32[32,72,256]{2,1,0:T(8,128)} %dynamic_update_slice.3), calls=%async_computation.1 | async-start | bytes 4718592 | tf_op jit(solution)/shard_map/all_to_all | solution.py:144
  130.2 0.7 fusion
  130.9 54.9 %all-to-all-done.1 = f32[32,72,256]{2,1,0:T(8,128)S(1)} async-done(((f32[32,72,256]{2,1,0:T(8,128)}), f32[32,72,256]{2,1,0:T(8,128)S(1)}, u32[]{:S(2)}, u32[]{:S(2)}) %all-to-all-start.1) | async-done | bytes 2359328 | tf_op jit(solution)/shard_map/all_to_all | solution.py:144
  187.9 1.2 compare_reduce_fusion.1
  189.5 0.7 fusion.1
  (42 shorter events, 6.6 us)
Async XLA Ops:
  0.6 49.1 %copy-start.6 = (s32[14]{0:T(128)S(1)}, s32[14]{0:T(128)}, u32[]{:S(2)}) copy-start(s32[14]{0:T(128)} %param.9) | copy-start | bytes 172
  0.6 49.1 %copy-start.5 = (s32[14]{0:T(128)S(1)}, s32[14]{0:T(128)}, u32[]{:S(2)}) copy-start(s32[14]{0:T(128)} %param.12) | copy-start | bytes 172
  0.7 50.4 %copy-start.3 = (s32[14]{0:T(128)S(1)}, s32[14]{0:T(128)}, u32[]{:S(2)}) copy-start(s32[14]{0:T(128)} %param.10) | copy-start | bytes 172
  0.7 50.4 %copy-start.4 = (s32[14]{0:T(128)S(1)}, s32[14]{0:T(128)}, u32[]{:S(2)}) copy-start(s32[14]{0:T(128)} %param.11) | copy-start | bytes 172
  0.7 16.3 %collective-permute-start = (bf16[128,256]{1,0:T(8,128)(2,1)}, bf16[128,256]{1,0:T(8,128)(2,1)S(1)}, u32[]{:S(2)}, u32[]{:S(2)}) collective-permute-start(bf16[128,256]{1,0:T(8,128)(2,1)} %param.13), channel_id=1, source_target_pairs={{0,4},{4,8},{8,12},{12,16},{16,20},{20,24},{24,28},{28,0},{1,5},{5... | collective-permute-start | bytes 196616 | tf_op jit(solution)/shard_map/ppermute | solution.py:117
  2.7 17.6 %collective-permute-start.1 = (bf16[128,256]{1,0:T(8,128)(2,1)}, bf16[128,256]{1,0:T(8,128)(2,1)S(1)}, u32[]{:S(2)}, u32[]{:S(2)}) collective-permute-start(bf16[128,256]{1,0:T(8,128)(2,1)} %param.13), channel_id=1, source_target_pairs={{0,8},{4,12},{8,16},{12,20},{16,24},{20,28},{24,0},{28,4},{1,9},{5... | collective-permute-start | bytes 196616 | tf_op jit(solution)/shard_map/ppermute | solution.py:117
  5.9 16.0 %collective-permute-start.2 = (bf16[128,256]{1,0:T(8,128)(2,1)}, bf16[128,256]{1,0:T(8,128)(2,1)S(1)}, u32[]{:S(2)}, u32[]{:S(2)}) collective-permute-start(bf16[128,256]{1,0:T(8,128)(2,1)} %param.13), channel_id=1, source_target_pairs={{0,12},{4,16},{8,20},{12,24},{16,28},{20,0},{24,4},{28,8},{1,13},{... | collective-permute-start | bytes 196616 | tf_op jit(solution)/shard_map/ppermute | solution.py:117
  10.0 12.6 %collective-permute-start.3 = (bf16[128,256]{1,0:T(8,128)(2,1)}, bf16[128,256]{1,0:T(8,128)(2,1)S(1)}, u32[]{:S(2)}, u32[]{:S(2)}) collective-permute-start(bf16[128,256]{1,0:T(8,128)(2,1)} %param.13), channel_id=1, source_target_pairs={{0,16},{4,20},{8,24},{12,28},{16,0},{20,4},{24,8},{28,12},{1,17},{... | collective-permute-start | bytes 196616 | tf_op jit(solution)/shard_map/ppermute | solution.py:117
  10.5 12.7 %collective-permute-start.4 = (bf16[128,256]{1,0:T(8,128)(2,1)}, bf16[128,256]{1,0:T(8,128)(2,1)S(1)}, u32[]{:S(2)}, u32[]{:S(2)}) collective-permute-start(bf16[128,256]{1,0:T(8,128)(2,1)} %param.13), channel_id=1, source_target_pairs={{0,20},{4,24},{8,28},{12,0},{16,4},{20,8},{24,12},{28,16},{1,21},{... | collective-permute-start | bytes 196616 | tf_op jit(solution)/shard_map/ppermute | solution.py:117
  17.0 7.8 %collective-permute-start.5 = (bf16[128,256]{1,0:T(8,128)(2,1)}, bf16[128,256]{1,0:T(8,128)(2,1)S(1)}, u32[]{:S(2)}, u32[]{:S(2)}) collective-permute-start(bf16[128,256]{1,0:T(8,128)(2,1)} %param.13), channel_id=1, source_target_pairs={{0,24},{4,28},{8,0},{12,4},{16,8},{20,12},{24,16},{28,20},{1,25},{... | collective-permute-start | bytes 196616 | tf_op jit(solution)/shard_map/ppermute | solution.py:117
  20.3 5.6 %collective-permute-start.6 = (bf16[128,256]{1,0:T(8,128)(2,1)}, bf16[128,256]{1,0:T(8,128)(2,1)S(1)}, u32[]{:S(2)}, u32[]{:S(2)}) collective-permute-start(bf16[128,256]{1,0:T(8,128)(2,1)} %param.13), channel_id=1, source_target_pairs={{0,28},{4,0},{8,4},{12,8},{16,12},{20,16},{24,20},{28,24},{1,29},{... | collective-permute-start | bytes 196616 | tf_op jit(solution)/shard_map/ppermute | solution.py:117
  26.5 18.5 %collective-permute-start.7 = (bf16[1024,256]{1,0:T(8,128)(2,1)}, bf16[1024,256]{1,0:T(8,128)(2,1)S(1)}, u32[]{:S(2)}, u32[]{:S(2)}) collective-permute-start(bf16[1024,256]{1,0:T(8,128)(2,1)} %get-tuple-element.17), channel_id=1, source_target_pairs={{0,1},{1,2},{2,3},{3,0},{4,5},{5,6},{6,7},{7,4},{8,9},{9,10},{10,1... | collective-permute-start | bytes 1572872 | tf_op jit(solution)/shard_map/ppermute | solution.py:117
  28.0 18.0 %collective-permute-start.9 = (bf16[1024,256]{1,0:T(8,128)(2,1)}, bf16[1024,256]{1,0:T(8,128)(2,1)S(1)}, u32[]{:S(2)}, u32[]{:S(2)}) collective-permute-start(bf16[1024,256]{1,0:T(8,128)(2,1)} %get-tuple-element.17), channel_id=1, source_target_pairs={{0,3},{1,0},{2,1},{3,2},{4,7},{5,4},{6,5},{7,6},{8,11},{9,8},{10,9... | collective-permute-start | bytes 1572872 | tf_op jit(solution)/shard_map/ppermute | solution.py:117
  45.7 10.0 %collective-permute-start.8 = (bf16[512,256]{1,0:T(8,128)(2,1)}, bf16[512,256]{1,0:T(8,128)(2,1)S(1)}, u32[]{:S(2)}, u32[]{:S(2)}) collective-permute-start(bf16[512,256]{1,0:T(8,128)(2,1)} %slice.37), channel_id=1, source_target_pairs={{0,1},{1,2},{2,3},{3,0},{4,5},{5,6},{6,7},{7,4},{8,9},{9,10},{10,1... | collective-permute-start | bytes 786440 | tf_op jit(solution)/shard_map/ppermute | solution.py:117
  46.7 9.1 %collective-permute-start.10 = (bf16[512,256]{1,0:T(8,128)(2,1)}, bf16[512,256]{1,0:T(8,128)(2,1)}, u32[]{:S(2)}, u32[]{:S(2)}) collective-permute-start(bf16[512,256]{1,0:T(8,128)(2,1)} %slice.38), channel_id=1, source_target_pairs={{0,3},{1,0},{2,1},{3,2},{4,7},{5,4},{6,5},{7,6},{8,11},{9,8},{10,9... | collective-permute-start | bytes 786440 | tf_op jit(solution)/shard_map/ppermute | solution.py:117
  56.8 1.3 copy-start
  123.2 7.0 %copy-start.1 = (bf16[128,256]{1,0:T(8,128)(2,1)S(1)}, bf16[128,256]{1,0:T(8,128)(2,1)}, u32[]{:S(2)}) copy-start(bf16[128,256]{1,0:T(8,128)(2,1)} %param.14) | copy-start | bytes 196612
  123.2 62.6 %all-to-all-start.1 = ((f32[32,72,256]{2,1,0:T(8,128)}), f32[32,72,256]{2,1,0:T(8,128)S(1)}, u32[]{:S(2)}, u32[]{:S(2)}) async-start(f32[32,72,256]{2,1,0:T(8,128)} %dynamic_update_slice.3), calls=%async_computation.1 | async-start | bytes 4718592 | tf_op jit(solution)/shard_map/all_to_all | solution.py:144
  130.2 59.3 %copy-start.2 = (bf16[128,256]{1,0:T(8,128)(2,1)S(1)}, bf16[128,256]{1,0:T(8,128)(2,1)}, u32[]{:S(2)}) copy-start(bf16[128,256]{1,0:T(8,128)(2,1)} %param.13) | copy-start | bytes 196612

commit v2 on v1

--- a/solution.py
+++ b/solution.py
@@ -8,7 +8,15 @@
 step_size = 0.05
 f32 = jnp.float32
 bf16 = jnp.bfloat16
+f16 = jnp.float16
+LANES = 128
+HEAD = 16
+TOP = 14
 GROUP = 8
+
+
+def power_of(size):
+    return jnp.ceil(jnp.log(jnp.maximum(size, 1e-30)) * (1.0 / 0.6931471805599453))
 
 
 def block_kernel(
@@ -57,8 +65,14 @@
             cols = jnp.sum(partial_sum.reshape(GROUP, side, width) * c_f[None], axis=1)
             at = (b_index, pl.ds(group * GROUP, GROUP), slice(None))
             b_grad_ref[at] = b_grad_ref[at] + cols
-        slots_ref[slot, pl.ds(0, side), :] = grad_rows
-        slots_ref[slot, pl.ds(side, 8), :] = jnp.full((8, width), tab[5, i].astype(f32), f32)
+        power = power_of(jnp.max(jnp.abs(grad_rows), axis=(0, 1), keepdims=True))
+        scaled = (grad_rows * jnp.exp2(TOP - power)).astype(slots_ref.dtype)
+        for part in range(width // LANES):
+            columns = slice(part * LANES, (part + 1) * LANES)
+            slots_ref[slot, pl.ds(part * side, side), :] = scaled[:, columns]
+        row = lax.broadcasted_iota(jnp.int32, (HEAD, LANES), 0)
+        head = jnp.where(row == 0, tab[5, i].astype(f32), jnp.where(row == 1, power, 0.0))
+        slots_ref[slot, pl.ds(side * width // LANES, HEAD), :] = head.astype(slots_ref.dtype)
 
     @pl.when(held != 0)
     def _():
@@ -88,7 +102,7 @@
             pl.BlockSpec((1, side, width), lambda i, tab: (tab[2, i], 0, 0)),
         ],
         out_specs=[
-            pl.BlockSpec((n_slots, side + 8, width), whole3),
+            pl.BlockSpec((n_slots, side * width // LANES + HEAD, LANES), whole3),
             pl.BlockSpec(b_panel.shape, whole3),
             pl.BlockSpec((8, 128), lambda i, tab: (0, 0)),
         ],
@@ -96,7 +110,7 @@
     return pl.pallas_call(
         block_kernel,
         out_shape=[
-            jax.ShapeDtypeStruct((n_slots, side + 8, width), f32),
+            jax.ShapeDtypeStruct((n_slots, side * width // LANES + HEAD, LANES), f32),
             jax.ShapeDtypeStruct(b_panel.shape, f32),
             jax.ShapeDtypeStruct((8, 128), f32),
         ],
@@ -139,14 +153,27 @@
     got = jnp.sum(lax.all_to_all(sent, grid_axes, 0, 0, tiled=True), axis=0)
     rows = factor_b.shape[0]
     grad_b = got[:rows]
-    group_totals = jnp.broadcast_to(got[None, rows : rows + 2], (n_wide, 2, width))
-    sent = lax.dynamic_update_slice(slots, group_totals, (0, side + 1, 0))
+    loss_group, held_group = got[rows, 0], got[rows + 1, 0]
+    loss_power = power_of(jnp.abs(loss_group))
+    fraction = loss_group * jnp.exp2(-loss_power)
+    lead = lax.reduce_precision(fraction, 5, 10)
+    rest = (fraction - lead) * 2048.0
+    head = jnp.stack([loss_power, lead, rest, held_group]).astype(f16)
+    head = jnp.broadcast_to(head[None, :, None], (n_wide, 4, LANES))
+    tall = side * width // LANES
+    sent = lax.dynamic_update_slice(slots.astype(f16), head, (0, tall + 2, 0))
     got = lax.all_to_all(sent, wide_axes, 0, 0, tiled=True)
-    which = got[:, side : side + 1, :1]
-    grad_a = jnp.concatenate(
-        [jnp.sum(jnp.where(which == k, got[:, :side], 0.0), axis=0) for k in range(own)]
-    )
-    totals = jnp.sum(got[:, side + 1 : side + 3, 0], axis=0)
+    heads = got[:, tall : tall + 6, 0].astype(f32)
+    which, scale = heads[:, 0], jnp.exp2(heads[:, 1] - TOP)
+    picked = jnp.where(which[None, :] == jnp.arange(own, dtype=f32)[:, None], scale[None, :], 0.0)
+    grads = got[:, :tall].astype(f32)
+    grad_a = jnp.stack([jnp.sum(picked[k][:, None, None] * grads, axis=0) for k in range(own)])
+    grad_a = grad_a.reshape(own, width // LANES, side, LANES).transpose(0, 2, 1, 3)
+    grad_a = grad_a.reshape(own * side, width)
+    totals = [
+        jnp.sum(jnp.exp2(heads[:, 2]) * (heads[:, 3] + heads[:, 4] / 2048.0)),
+        jnp.sum(heads[:, 5]),
+    ]
     held_loss = totals[0] / (totals[1] * (side * side * side))
     next_a = factor_a.astype(f32) - step_size * grad_a
     next_b = factor_b.astype(f32) - step_size * grad_b

time: 193 us -> 173 us (0.90)
  waiting for transfers between devices: 60.4 us -> 18.9 us
  blocking collectives: 35.8 us -> 55.9 us
  between operations: 3.88 us -> 7.73 us
  starting transfers between devices: 31.9 us -> 29.4 us
    all_to_all x1, waiting for transfers between devices: 54.9 us -> 13.4 us  [step(): got = jnp.sum(lax.all_to_all(sent, grid_axes, 0, 0, tiled=True), axis=0)]
    all_to_all x1, blocking collectives: 21.2 us -> 41.3 us  [step(): got = lax.all_to_all(sent, wide_axes, 0, 0, tiled=True)]
    all_to_all x1, starting transfers between devices: 6.99 us -> 4.5 us  [step(): got = jnp.sum(lax.all_to_all(sent, grid_axes, 0, 0, tiled=True), axis=0)]
  transfers between devices with their start and end apart: 12 -> 12, of which waited for: 5 -> 5; matrix products, arithmetic and copies ran while one was open for 5% -> 6% of each run, Pallas kernels for 0% -> 0%
where the time goes in v2:
time: 173 us; the launch traced here: 172 us
  blocking collectives  55.9 us (32%)
  Pallas kernels  38.8 us (22%)
  starting transfers between devices  29.4 us (17%)
  waiting for transfers between devices  18.9 us (11%)
  local copies, waits for them, and re-layouts  11.5 us (7%)
  other arithmetic  9.58 us (6%)
  between operations  7.73 us (4%)
    all_to_all x1, blocking collectives, step(): got = lax.all_to_all(sent, wide_axes, 0, 0, tiled=True)  41.3 us
    pallas_call x1, Pallas kernels, run_blocks(): pl.pallas_call(block_kernel, out_shape=[jax.ShapeDtypeStruct((n_slots, si...  38.8 us
    ppermute x11, starting transfers between devices, shift(): return lax.ppermute(v, axis, [(k, (k + by) % n) for k in range(n)])  24.9 us
    all_gather x1, blocking collectives, step(): lax.all_gather(factor_b, grid_axes, axis=0, tiled=True)  14.6 us
    all_to_all x1, waiting for transfers between devices, step(): got = jnp.sum(lax.all_to_all(sent, grid_axes, 0, 0, tiled=True), axis=0)  13.4 us
    unnamed x24, local copies, waits for them, and re-layouts  7.63 us
    ppermute x11, waiting for transfers between devices, shift(): return lax.ppermute(v, axis, [(k, (k + by) % n) for k in range(n)])  5.46 us
    all_to_all x1, starting transfers between devices, step(): got = jnp.sum(lax.all_to_all(sent, grid_axes, 0, 0, tiled=True), axis=0)  4.5 us
  transfers between devices with their start and end apart: 12, of which 5 were waited for; matrix products, arithmetic and copies ran while one was open for 6% of the time, Pallas kernels for 0%

profile of v2, /device:TPU:8, one launch (start us, length us, event | category | flops | bytes accessed | tf_op | source)
XLA Modules:
  0.0 171.9 jit_solution(14285710536532210567)
XLA Ops:
  0.7 2.0 %collective-permute-start = (bf16[128,256]{1,0:T(8,128)(2,1)}, bf16[128,256]{1,0:T(8,128)(2,1)S(1)}, u32[]{:S(2)}, u32[]{:S(2)}) collective-permute-start(bf16[128,256]{1,0:T(8,128)(2,1)} %param.13), channel_id=1, source_target_pairs={{0,4},{4,8},{8,12},{12,16},{16,20},{20,24},{24,28},{28,0},{1,5},{5... | collective-permute-start | bytes 196616 | tf_op jit(solution)/shard_map/ppermute | solution.py:131
  2.7 3.3 %collective-permute-start.1 = (bf16[128,256]{1,0:T(8,128)(2,1)}, bf16[128,256]{1,0:T(8,128)(2,1)S(1)}, u32[]{:S(2)}, u32[]{:S(2)}) collective-permute-start(bf16[128,256]{1,0:T(8,128)(2,1)} %param.13), channel_id=1, source_target_pairs={{0,8},{4,12},{8,16},{12,20},{16,24},{20,28},{24,0},{28,4},{1,9},{5... | collective-permute-start | bytes 196616 | tf_op jit(solution)/shard_map/ppermute | solution.py:131
  5.9 4.0 %collective-permute-start.2 = (bf16[128,256]{1,0:T(8,128)(2,1)}, bf16[128,256]{1,0:T(8,128)(2,1)S(1)}, u32[]{:S(2)}, u32[]{:S(2)}) collective-permute-start(bf16[128,256]{1,0:T(8,128)(2,1)} %param.13), channel_id=1, source_target_pairs={{0,12},{4,16},{8,20},{12,24},{16,28},{20,0},{24,4},{28,8},{1,13},{... | collective-permute-start | bytes 196616 | tf_op jit(solution)/shard_map/ppermute | solution.py:131
  10.5 4.9 %collective-permute-start.4 = (bf16[128,256]{1,0:T(8,128)(2,1)}, bf16[128,256]{1,0:T(8,128)(2,1)S(1)}, u32[]{:S(2)}, u32[]{:S(2)}) collective-permute-start(bf16[128,256]{1,0:T(8,128)(2,1)} %param.13), channel_id=1, source_target_pairs={{0,20},{4,24},{8,28},{12,0},{16,4},{20,8},{24,12},{28,16},{1,21},{... | collective-permute-start | bytes 196616 | tf_op jit(solution)/shard_map/ppermute | solution.py:131
  15.5 1.5 constant_dynamic-update-slice_fusion.7
  17.0 2.7 %collective-permute-start.5 = (bf16[128,256]{1,0:T(8,128)(2,1)}, bf16[128,256]{1,0:T(8,128)(2,1)S(1)}, u32[]{:S(2)}, u32[]{:S(2)}) collective-permute-start(bf16[128,256]{1,0:T(8,128)(2,1)} %param.13), channel_id=1, source_target_pairs={{0,24},{4,28},{8,0},{12,4},{16,8},{20,12},{24,16},{28,20},{1,25},{... | collective-permute-start | bytes 196616 | tf_op jit(solution)/shard_map/ppermute | solution.py:131
  19.6 0.6 constant_dynamic-update-slice_fusion.6
  20.3 1.0 collective-permute-start.6
  22.5 0.6 constant_dynamic-update-slice_fusion.3
  23.2 0.6 constant_dynamic-update-slice_fusion.2
  23.8 1.0 collective-permute-done.5
  26.5 1.5 collective-permute-start.7
  28.0 1.7 %collective-permute-start.9 = (bf16[1024,256]{1,0:T(8,128)(2,1)}, bf16[1024,256]{1,0:T(8,128)(2,1)S(1)}, u32[]{:S(2)}, u32[]{:S(2)}) collective-permute-start(bf16[1024,256]{1,0:T(8,128)(2,1)} %get-tuple-element.19), channel_id=1, source_target_pairs={{0,3},{1,0},{2,1},{3,2},{4,7},{5,4},{6,5},{7,6},{8,11},{9,8},{10,9... | collective-permute-start | bytes 1572872 | tf_op jit(solution)/shard_map/ppermute | solution.py:131
  29.7 0.7 fusion.9
  30.4 14.6 %all_gather.3 = bf16[1024,256]{1,0:T(8,128)(2,1)} all-gather(bf16[128,256]{1,0:T(8,128)(2,1)} %param.14), channel_id=1, replica_groups=mesh['y'=4,'core'=2,'z'=8,'x'=4] {'y','core'}, dimensions={0}, use_global_device_ids=true | all-gather | bytes 589824 | tf_op jit(solution)/shard_map/all_gather | solution.py:134
  45.0 0.7 slice.61
  46.0 0.7 slice.62
  46.7 3.0 %collective-permute-start.10 = (bf16[512,256]{1,0:T(8,128)(2,1)}, bf16[512,256]{1,0:T(8,128)(2,1)}, u32[]{:S(2)}, u32[]{:S(2)}) collective-permute-start(bf16[512,256]{1,0:T(8,128)(2,1)} %slice.62), channel_id=1, source_target_pairs={{0,3},{1,0},{2,1},{3,2},{4,7},{5,4},{6,5},{7,6},{8,11},{9,8},{10,9... | collective-permute-start | bytes 786440 | tf_op jit(solution)/shard_map/ppermute | solution.py:131
  49.7 0.6 reduce_sum.64
  51.7 4.0 %collective-permute-done.8 = bf16[512,256]{1,0:T(8,128)(2,1)S(1)} collective-permute-done((bf16[512,256]{1,0:T(8,128)(2,1)}, bf16[512,256]{1,0:T(8,128)(2,1)S(1)}, u32[]{:S(2)}, u32[]{:S(2)}) %collective-permute-start.8) | collective-permute-done | bytes 262176 | tf_op jit(solution)/shard_map/ppermute | solution.py:131
  55.8 1.0 constant_dynamic-update-slice_fusion.9
  56.8 1.3 copy-done
  58.1 38.8 %shard_map.103 = (f32[32,144,128]{2,1,0:T(8,128)}, f32[16,64,256]{2,1,0:T(8,128)}, f32[8,128]{1,0:T(8,128)}) custom-call(s32[6,14]{1,0:T(8,128)} %stack.59.tab, bf16[14,64,4096]{2,1,0:T(8,128)(2,1)} %values_ref.1, bf16[64,64,256]{2,1,0:T(8,128)(2,1)} %bitcast.36, bf16[16,64,256]{2,1,0:T(8,128)(2,1)} %bitcast.37, bf16[64,64,256]{2,1,0:T(8,128)(2,1)} %bitcast.38), custom_call_target="tpu_custom_call" | custom-call | tf_op jit(solution)/shard_map/pallas_call | solution.py:110
  97.0 1.3 reduce_sum.63
  98.3 0.7 pad_maximum_fusion
  99.0 2.4 %maximum_maximum_fusion = f32[8,136,256]{2,1,0:T(8,128)} fusion(f32[8,128,256]{2,1,0:T(8,128)} %bitcast.39, f32[136]{0:T(256)S(1)} %pad.8.clone, f32[136]{0:T(256)S(1)} %pad_maximum_fusion), kind=kLoop, calls=%fused_computation.4 | loop fusion | flops 557056 | bytes 2163776 | tf_op jit(solution)/shard_map/concatenate | solution.py:152
  101.4 4.5 %all-to-all-start = ((f32[8,136,256]{2,1,0:T(8,128)}), f32[8,136,256]{2,1,0:T(8,128)S(1)}, u32[]{:S(2)}, u32[]{:S(2)}) async-start(f32[8,136,256]{2,1,0:T(8,128)} %maximum_maximum_fusion), calls=%async_computation | async-start | bytes 2228224 | tf_op jit(solution)/shard_map/all_to_all | solution.py:153
  105.9 1.8 %convert_element_type.27 = f16[32,144,128]{2,1,0:T(8,128)(2,1)S(1)} convert(f32[32,144,128]{2,1,0:T(8,128)} %get-tuple-element.6) | non-fusion elementwise | flops 589824 | bytes 3538944 | tf_op jit(solution)/shard_map/convert_element_type | solution.py:164
  107.7 13.4 %all-to-all-done = f32[8,136,256]{2,1,0:T(8,128)S(1)} async-done(((f32[8,136,256]{2,1,0:T(8,128)}), f32[8,136,256]{2,1,0:T(8,128)S(1)}, u32[]{:S(2)}, u32[]{:S(2)}) %all-to-all-start) | async-done | bytes 1114144 | tf_op jit(solution)/shard_map/all_to_all | solution.py:153
  126.0 41.3 %all_to_all.10 = f16[32,144,128]{2,1,0:T(8,128)(2,1)S(1)} all-to-all(f16[32,144,128]{2,1,0:T(8,128)(2,1)S(1)} %dynamic_update_slice.3), channel_id=1, replica_groups=mesh['y'=4,'core'=2,'z'=8,'x'=4] {'z','x'}, dimensions={0} | all-to-all | bytes 2359296 | tf_op jit(solution)/shard_map/all_to_all | solution.py:165
  167.5 0.7 slice_reduce_fusion
  168.8 0.7 bitcast_subtract_fusion
  (47 shorter events, 6.4 us)
Async XLA Ops:
  0.6 49.1 %copy-start.6 = (s32[14]{0:T(128)S(1)}, s32[14]{0:T(128)}, u32[]{:S(2)}) copy-start(s32[14]{0:T(128)} %param.9) | copy-start | bytes 172
  0.6 49.1 %copy-start.5 = (s32[14]{0:T(128)S(1)}, s32[14]{0:T(128)}, u32[]{:S(2)}) copy-start(s32[14]{0:T(128)} %param.12) | copy-start | bytes 172
  0.7 50.4 %copy-start.3 = (s32[14]{0:T(128)S(1)}, s32[14]{0:T(128)}, u32[]{:S(2)}) copy-start(s32[14]{0:T(128)} %param.10) | copy-start | bytes 172
  0.7 50.4 %copy-start.4 = (s32[14]{0:T(128)S(1)}, s32[14]{0:T(128)}, u32[]{:S(2)}) copy-start(s32[14]{0:T(128)} %param.11) | copy-start | bytes 172
  0.7 16.3 %collective-permute-start = (bf16[128,256]{1,0:T(8,128)(2,1)}, bf16[128,256]{1,0:T(8,128)(2,1)S(1)}, u32[]{:S(2)}, u32[]{:S(2)}) collective-permute-start(bf16[128,256]{1,0:T(8,128)(2,1)} %param.13), channel_id=1, source_target_pairs={{0,4},{4,8},{8,12},{12,16},{16,20},{20,24},{24,28},{28,0},{1,5},{5... | collective-permute-start | bytes 196616 | tf_op jit(solution)/shard_map/ppermute | solution.py:131
  2.7 17.6 %collective-permute-start.1 = (bf16[128,256]{1,0:T(8,128)(2,1)}, bf16[128,256]{1,0:T(8,128)(2,1)S(1)}, u32[]{:S(2)}, u32[]{:S(2)}) collective-permute-start(bf16[128,256]{1,0:T(8,128)(2,1)} %param.13), channel_id=1, source_target_pairs={{0,8},{4,12},{8,16},{12,20},{16,24},{20,28},{24,0},{28,4},{1,9},{5... | collective-permute-start | bytes 196616 | tf_op jit(solution)/shard_map/ppermute | solution.py:131
  5.9 16.0 %collective-permute-start.2 = (bf16[128,256]{1,0:T(8,128)(2,1)}, bf16[128,256]{1,0:T(8,128)(2,1)S(1)}, u32[]{:S(2)}, u32[]{:S(2)}) collective-permute-start(bf16[128,256]{1,0:T(8,128)(2,1)} %param.13), channel_id=1, source_target_pairs={{0,12},{4,16},{8,20},{12,24},{16,28},{20,0},{24,4},{28,8},{1,13},{... | collective-permute-start | bytes 196616 | tf_op jit(solution)/shard_map/ppermute | solution.py:131
  10.0 12.6 %collective-permute-start.3 = (bf16[128,256]{1,0:T(8,128)(2,1)}, bf16[128,256]{1,0:T(8,128)(2,1)S(1)}, u32[]{:S(2)}, u32[]{:S(2)}) collective-permute-start(bf16[128,256]{1,0:T(8,128)(2,1)} %param.13), channel_id=1, source_target_pairs={{0,16},{4,20},{8,24},{12,28},{16,0},{20,4},{24,8},{28,12},{1,17},{... | collective-permute-start | bytes 196616 | tf_op jit(solution)/shard_map/ppermute | solution.py:131
  10.5 12.7 %collective-permute-start.4 = (bf16[128,256]{1,0:T(8,128)(2,1)}, bf16[128,256]{1,0:T(8,128)(2,1)S(1)}, u32[]{:S(2)}, u32[]{:S(2)}) collective-permute-start(bf16[128,256]{1,0:T(8,128)(2,1)} %param.13), channel_id=1, source_target_pairs={{0,20},{4,24},{8,28},{12,0},{16,4},{20,8},{24,12},{28,16},{1,21},{... | collective-permute-start | bytes 196616 | tf_op jit(solution)/shard_map/ppermute | solution.py:131
  17.0 7.8 %collective-permute-start.5 = (bf16[128,256]{1,0:T(8,128)(2,1)}, bf16[128,256]{1,0:T(8,128)(2,1)S(1)}, u32[]{:S(2)}, u32[]{:S(2)}) collective-permute-start(bf16[128,256]{1,0:T(8,128)(2,1)} %param.13), channel_id=1, source_target_pairs={{0,24},{4,28},{8,0},{12,4},{16,8},{20,12},{24,16},{28,20},{1,25},{... | collective-permute-start | bytes 196616 | tf_op jit(solution)/shard_map/ppermute | solution.py:131
  20.3 5.6 %collective-permute-start.6 = (bf16[128,256]{1,0:T(8,128)(2,1)}, bf16[128,256]{1,0:T(8,128)(2,1)S(1)}, u32[]{:S(2)}, u32[]{:S(2)}) collective-permute-start(bf16[128,256]{1,0:T(8,128)(2,1)} %param.13), channel_id=1, source_target_pairs={{0,28},{4,0},{8,4},{12,8},{16,12},{20,16},{24,20},{28,24},{1,29},{... | collective-permute-start | bytes 196616 | tf_op jit(solution)/shard_map/ppermute | solution.py:131
  26.5 18.5 %collective-permute-start.7 = (bf16[1024,256]{1,0:T(8,128)(2,1)}, bf16[1024,256]{1,0:T(8,128)(2,1)S(1)}, u32[]{:S(2)}, u32[]{:S(2)}) collective-permute-start(bf16[1024,256]{1,0:T(8,128)(2,1)} %get-tuple-element.19), channel_id=1, source_target_pairs={{0,1},{1,2},{2,3},{3,0},{4,5},{5,6},{6,7},{7,4},{8,9},{9,10},{10,1... | collective-permute-start | bytes 1572872 | tf_op jit(solution)/shard_map/ppermute | solution.py:131
  28.0 18.0 %collective-permute-start.9 = (bf16[1024,256]{1,0:T(8,128)(2,1)}, bf16[1024,256]{1,0:T(8,128)(2,1)S(1)}, u32[]{:S(2)}, u32[]{:S(2)}) collective-permute-start(bf16[1024,256]{1,0:T(8,128)(2,1)} %get-tuple-element.19), channel_id=1, source_target_pairs={{0,3},{1,0},{2,1},{3,2},{4,7},{5,4},{6,5},{7,6},{8,11},{9,8},{10,9... | collective-permute-start | bytes 1572872 | tf_op jit(solution)/shard_map/ppermute | solution.py:131
  45.7 10.0 %collective-permute-start.8 = (bf16[512,256]{1,0:T(8,128)(2,1)}, bf16[512,256]{1,0:T(8,128)(2,1)S(1)}, u32[]{:S(2)}, u32[]{:S(2)}) collective-permute-start(bf16[512,256]{1,0:T(8,128)(2,1)} %slice.61), channel_id=1, source_target_pairs={{0,1},{1,2},{2,3},{3,0},{4,5},{5,6},{6,7},{7,4},{8,9},{9,10},{10,1... | collective-permute-start | bytes 786440 | tf_op jit(solution)/shard_map/ppermute | solution.py:131
  46.7 9.1 %collective-permute-start.10 = (bf16[512,256]{1,0:T(8,128)(2,1)}, bf16[512,256]{1,0:T(8,128)(2,1)}, u32[]{:S(2)}, u32[]{:S(2)}) collective-permute-start(bf16[512,256]{1,0:T(8,128)(2,1)} %slice.62), channel_id=1, source_target_pairs={{0,3},{1,0},{2,1},{3,2},{4,7},{5,4},{6,5},{7,6},{8,11},{9,8},{10,9... | collective-permute-start | bytes 786440 | tf_op jit(solution)/shard_map/ppermute | solution.py:131
  56.8 1.3 copy-start
  101.4 19.7 %all-to-all-start = ((f32[8,136,256]{2,1,0:T(8,128)}), f32[8,136,256]{2,1,0:T(8,128)S(1)}, u32[]{:S(2)}, u32[]{:S(2)}) async-start(f32[8,136,256]{2,1,0:T(8,128)} %maximum_maximum_fusion), calls=%async_computation | async-start | bytes 2228224 | tf_op jit(solution)/shard_map/all_to_all | solution.py:153
  126.0 42.7 %copy-start.1 = (bf16[128,256]{1,0:T(8,128)(2,1)S(1)}, bf16[128,256]{1,0:T(8,128)(2,1)}, u32[]{:S(2)}) copy-start(bf16[128,256]{1,0:T(8,128)(2,1)} %param.13) | copy-start | bytes 196612
  126.0 42.7 %copy-start.2 = (bf16[128,256]{1,0:T(8,128)(2,1)S(1)}, bf16[128,256]{1,0:T(8,128)(2,1)}, u32[]{:S(2)}) copy-start(bf16[128,256]{1,0:T(8,128)(2,1)} %param.14) | copy-start | bytes 196612

commit v3 on v2

--- a/solution.py
+++ b/solution.py
@@ -88,6 +88,19 @@
             lanes = lanes + folded[:, k * 128 : (k + 1) * 128]
         loss_ref[...] = loss_ref[...] + lanes
 
+    @pl.when(i == pl.num_programs(0) - 1)
+    def _():
+        loss = jnp.sum(loss_ref[...], axis=(0, 1), keepdims=True)
+        power = power_of(jnp.abs(loss))
+        fraction = loss * jnp.exp2(-power)
+        lead = fraction.astype(bf16).astype(f32)
+        row = lax.broadcasted_iota(jnp.int32, (HEAD, LANES), 0)
+        head = jnp.where(row == 5, tab[6, 0].astype(f32), 0.0)
+        for k, part in ((2, power), (3, lead), (4, (fraction - lead) * 256.0)):
+            head = jnp.where(row == k, part, head)
+        at = (slice(None), pl.ds(side * width // LANES, HEAD), slice(None))
+        slots_ref[at] = slots_ref[at] + head[None]
+
 
 def run_blocks(table, values, a_panel, b_panel, c_panel, n_slots):
     side, width = a_panel.shape[1:]
@@ -104,15 +117,14 @@
         out_specs=[
             pl.BlockSpec((n_slots, side * width // LANES + HEAD, LANES), whole3),
             pl.BlockSpec(b_panel.shape, whole3),
-            pl.BlockSpec((8, 128), lambda i, tab: (0, 0)),
         ],
+        scratch_shapes=[pltpu.VMEM((8, LANES), f32)],
     )
     return pl.pallas_call(
         block_kernel,
         out_shape=[
             jax.ShapeDtypeStruct((n_slots, side * width // LANES + HEAD, LANES), f32),
             jax.ShapeDtypeStruct(b_panel.shape, f32),
-            jax.ShapeDtypeStruct((8, 128), f32),
         ],
         grid_spec=grid_spec,
     )(table, values, a_panel, b_panel, c_panel)
@@ -143,26 +155,19 @@
     within = a_block % own
     s = (z - holder // nx) % nz
     q = (x - holder % nx) % nx
-    table = jnp.stack([(q * nz + s) * own + within, b_block, c_block, held, holder, within])
-    slots, b_grad, loss = run_blocks(table, values, a_panel, b_panel, c_panel, n_wide)
+    held_count = jnp.full_like(held, jnp.sum(held))
+    table = jnp.stack([(q * nz + s) * own + within, b_block, c_block, held, holder, within, held_count])
+    slots, b_grad = run_blocks(table, values, a_panel, b_panel, c_panel, n_wide)
 
-    totals = jnp.stack([jnp.sum(loss), jnp.sum(held).astype(f32)])
-    extra = jnp.broadcast_to(totals[None, :, None], (n_grid, 2, width))
-    extra = jnp.concatenate([extra, jnp.zeros((n_grid, 6, width), f32)], axis=1)
-    sent = jnp.concatenate([b_grad.reshape(n_grid, -1, width), extra], axis=1)
-    got = jnp.sum(lax.all_to_all(sent, grid_axes, 0, 0, tiled=True), axis=0)
-    rows = factor_b.shape[0]
-    grad_b = got[:rows]
-    loss_group, held_group = got[rows, 0], got[rows + 1, 0]
-    loss_power = power_of(jnp.abs(loss_group))
-    fraction = loss_group * jnp.exp2(-loss_power)
-    lead = lax.reduce_precision(fraction, 5, 10)
-    rest = (fraction - lead) * 2048.0
-    head = jnp.stack([loss_power, lead, rest, held_group]).astype(f16)
-    head = jnp.broadcast_to(head[None, :, None], (n_wide, 4, LANES))
     tall = side * width // LANES
-    sent = lax.dynamic_update_slice(slots.astype(f16), head, (0, tall + 2, 0))
-    got = lax.all_to_all(sent, wide_axes, 0, 0, tiled=True)
+    packed, b_grad = lax.optimization_barrier((slots.astype(f16), b_grad))
+    got = lax.all_to_all(packed, wide_axes, 0, 0, tiled=True)
+    parts = b_grad.reshape(n_grid, -1, width)
+    me = lax.axis_index(grid_axes)
+    grad_b = lax.dynamic_index_in_dim(parts, me, 0, keepdims=False)
+    for by in range(1, n_grid):
+        part = lax.dynamic_index_in_dim(parts, (me + by) % n_grid, 0, keepdims=False)
+        grad_b = grad_b + shift(part, grid_axes, by)
     heads = got[:, tall : tall + 6, 0].astype(f32)
     which, scale = heads[:, 0], jnp.exp2(heads[:, 1] - TOP)
     picked = jnp.where(which[None, :] == jnp.arange(own, dtype=f32)[:, None], scale[None, :], 0.0)
@@ -170,10 +175,10 @@
     grad_a = jnp.stack([jnp.sum(picked[k][:, None, None] * grads, axis=0) for k in range(own)])
     grad_a = grad_a.reshape(own, width // LANES, side, LANES).transpose(0, 2, 1, 3)
     grad_a = grad_a.reshape(own * side, width)
-    totals = [
-        jnp.sum(jnp.exp2(heads[:, 2]) * (heads[:, 3] + heads[:, 4] / 2048.0)),
-        jnp.sum(heads[:, 5]),
-    ]
+    loss = jnp.sum(jnp.exp2(heads[:, 2]) * (heads[:, 3] + heads[:, 4] / 256.0))
+    totals = jnp.concatenate([jnp.full((4, LANES), loss), jnp.full((4, LANES), jnp.sum(heads[:, 5]))])
+    totals = jnp.broadcast_to(totals[None], (n_grid, 8, LANES))
+    totals = jnp.sum(lax.all_to_all(totals, grid_axes, 0, 0, tiled=True), axis=0)[::4, 0]
     held_loss = totals[0] / (totals[1] * (side * side * side))
     next_a = factor_a.astype(f32) - step_size * grad_a
     next_b = factor_b.astype(f32) - step_size * grad_b

time: 173 us -> 155 us (0.90)
  blocking collectives: 55.9 us -> 14.6 us
  starting transfers between devices: 29.4 us -> 49.5 us
  waiting for transfers between devices: 18.9 us -> 26.8 us
  between operations: 7.73 us -> 3.42 us
  local copies, waits for them, and re-layouts: 11.5 us -> 14 us
  other arithmetic: 9.58 us -> 7.67 us
    all_to_all x1 -> x0, blocking collectives: 41.3 us -> none  [step(): got = lax.all_to_all(sent, wide_axes, 0, 0, tiled=True)]
    all_to_all x1 -> x2, starting transfers between devices: 4.5 us -> 14.9 us  [the longest x1 10.6 us: step(): got = lax.all_to_all(packed, wide_axes, 0, 0, tiled=True)]
    ppermute x11 -> x18, starting transfers between devices: 24.9 us -> 34.6 us  [shift(): return lax.ppermute(v, axis, [(k, (k + by) % n) for k in range(n)])]
    ppermute x11 -> x18, waiting for transfers between devices: 5.46 us -> 9.96 us  [shift(): return lax.ppermute(v, axis, [(k, (k + by) % n) for k in range(n)])]
    all_to_all x1 -> x2, waiting for transfers between devices: 13.4 us -> 16.8 us  [the longest x1 14.1 us: step(): got = lax.all_to_all(packed, wide_axes, 0, 0, tiled=True)]
    concatenate x1 -> x0, other arithmetic: 2.41 us -> none  [step(): sent = jnp.concatenate([b_grad.reshape(n_grid, -1, width), extra], axis=1)]
    sub x0 -> x1, other arithmetic: none -> 1.76 us  [step(): next_b = factor_b.astype(f32) - step_size * grad_b]
    unnamed x24 -> x26, local copies, waits for them, and re-layouts: 7.63 us -> 7.69 us
  transfers between devices with their start and end apart: 12 -> 20, of which waited for: 5 -> 10; matrix products, arithmetic and copies ran while one was open for 6% -> 8% of each run, Pallas kernels for 0% -> 0%
where the time goes in v3:
time: 155 us; the launch traced here: 153 us
  starting transfers between devices  49.5 us (32%)
  Pallas kernels  37.5 us (24%)
  waiting for transfers between devices  26.8 us (17%)
  blocking collectives  14.6 us (9%)
  local copies, waits for them, and re-layouts  14 us (9%)
  other arithmetic  7.67 us (5%)
  between operations  3.42 us (2%)
    pallas_call x1, Pallas kernels, run_blocks(): pl.pallas_call(block_kernel, out_shape=[jax.ShapeDtypeStruct((n_slots, si...  37.5 us
    ppermute x18, starting transfers between devices, shift(): return lax.ppermute(v, axis, [(k, (k + by) % n) for k in range(n)])  34.6 us
    all_gather x1, blocking collectives, step(): lax.all_gather(factor_b, grid_axes, axis=0, tiled=True)  14.6 us
    all_to_all x1, waiting for transfers between devices, step(): got = lax.all_to_all(packed, wide_axes, 0, 0, tiled=True)  14.1 us
    all_to_all x1, starting transfers between devices, step(): got = lax.all_to_all(packed, wide_axes, 0, 0, tiled=True)  10.6 us
    ppermute x18, waiting for transfers between devices, shift(): return lax.ppermute(v, axis, [(k, (k + by) % n) for k in range(n)])  9.96 us
    unnamed x26, local copies, waits for them, and re-layouts  7.69 us
    all_to_all x1, starting transfers between devices, step(): lax.all_to_all(totals, grid_axes, 0, 0, tiled=True)  4.29 us
  transfers between devices with their start and end apart: 20, of which 10 were waited for; matrix products, arithmetic and copies ran while one was open for 8% of the time, Pallas kernels for 0%

profile of v3, /device:TPU:8, one launch (start us, length us, event | category | flops | bytes accessed | tf_op | source)
XLA Modules:
  0.0 153.4 jit_solution(9308291404483645836)
XLA Ops:
  0.7 2.0 %collective-permute-start = (bf16[128,256]{1,0:T(8,128)(2,1)}, bf16[128,256]{1,0:T(8,128)(2,1)S(1)}, u32[]{:S(2)}, u32[]{:S(2)}) collective-permute-start(bf16[128,256]{1,0:T(8,128)(2,1)} %param.13), channel_id=1, source_target_pairs={{0,4},{4,8},{8,12},{12,16},{16,20},{20,24},{24,28},{28,0},{1,5},{5... | collective-permute-start | bytes 196616 | tf_op jit(solution)/shard_map/ppermute | solution.py:143
  2.7 3.3 %collective-permute-start.1 = (bf16[128,256]{1,0:T(8,128)(2,1)}, bf16[128,256]{1,0:T(8,128)(2,1)S(1)}, u32[]{:S(2)}, u32[]{:S(2)}) collective-permute-start(bf16[128,256]{1,0:T(8,128)(2,1)} %param.13), channel_id=1, source_target_pairs={{0,8},{4,12},{8,16},{12,20},{16,24},{20,28},{24,0},{28,4},{1,9},{5... | collective-permute-start | bytes 196616 | tf_op jit(solution)/shard_map/ppermute | solution.py:143
  5.9 4.0 %collective-permute-start.2 = (bf16[128,256]{1,0:T(8,128)(2,1)}, bf16[128,256]{1,0:T(8,128)(2,1)S(1)}, u32[]{:S(2)}, u32[]{:S(2)}) collective-permute-start(bf16[128,256]{1,0:T(8,128)(2,1)} %param.13), channel_id=1, source_target_pairs={{0,12},{4,16},{8,20},{12,24},{16,28},{20,0},{24,4},{28,8},{1,13},{... | collective-permute-start | bytes 196616 | tf_op jit(solution)/shard_map/ppermute | solution.py:143
  10.5 4.9 %collective-permute-start.4 = (bf16[128,256]{1,0:T(8,128)(2,1)}, bf16[128,256]{1,0:T(8,128)(2,1)S(1)}, u32[]{:S(2)}, u32[]{:S(2)}) collective-permute-start(bf16[128,256]{1,0:T(8,128)(2,1)} %param.13), channel_id=1, source_target_pairs={{0,20},{4,24},{8,28},{12,0},{16,4},{20,8},{24,12},{28,16},{1,21},{... | collective-permute-start | bytes 196616 | tf_op jit(solution)/shard_map/ppermute | solution.py:143
  15.5 1.5 constant_dynamic-update-slice_fusion.7
  17.0 2.7 %collective-permute-start.5 = (bf16[128,256]{1,0:T(8,128)(2,1)}, bf16[128,256]{1,0:T(8,128)(2,1)S(1)}, u32[]{:S(2)}, u32[]{:S(2)}) collective-permute-start(bf16[128,256]{1,0:T(8,128)(2,1)} %param.13), channel_id=1, source_target_pairs={{0,24},{4,28},{8,0},{12,4},{16,8},{20,12},{24,16},{28,20},{1,25},{... | collective-permute-start | bytes 196616 | tf_op jit(solution)/shard_map/ppermute | solution.py:143
  20.3 1.0 collective-permute-start.6
  23.8 0.9 collective-permute-done.5
  26.5 1.5 collective-permute-start.7
  28.0 1.7 %collective-permute-start.9 = (bf16[1024,256]{1,0:T(8,128)(2,1)}, bf16[1024,256]{1,0:T(8,128)(2,1)S(1)}, u32[]{:S(2)}, u32[]{:S(2)}) collective-permute-start(bf16[1024,256]{1,0:T(8,128)(2,1)} %get-tuple-element.26), channel_id=1, source_target_pairs={{0,3},{1,0},{2,1},{3,2},{4,7},{5,4},{6,5},{7,6},{8,11},{9,8},{10,9... | collective-permute-start | bytes 1572872 | tf_op jit(solution)/shard_map/ppermute | solution.py:143
  30.4 14.6 %all_gather.3 = bf16[1024,256]{1,0:T(8,128)(2,1)} all-gather(bf16[128,256]{1,0:T(8,128)(2,1)} %param.14), channel_id=1, replica_groups=mesh['y'=4,'core'=2,'z'=8,'x'=4] {'y','core'}, dimensions={0}, use_global_device_ids=true | all-gather | bytes 589824 | tf_op jit(solution)/shard_map/all_gather | solution.py:146
  45.0 0.7 slice.62
  46.0 0.7 slice.63
  46.8 3.0 %collective-permute-start.10 = (bf16[512,256]{1,0:T(8,128)(2,1)}, bf16[512,256]{1,0:T(8,128)(2,1)}, u32[]{:S(2)}, u32[]{:S(2)}) collective-permute-start(bf16[512,256]{1,0:T(8,128)(2,1)} %slice.63), channel_id=1, source_target_pairs={{0,3},{1,0},{2,1},{3,2},{4,7},{5,4},{6,5},{7,6},{8,11},{9,8},{10,9... | collective-permute-start | bytes 786440 | tf_op jit(solution)/shard_map/ppermute | solution.py:143
  51.7 4.0 %collective-permute-done.8 = bf16[512,256]{1,0:T(8,128)(2,1)S(1)} collective-permute-done((bf16[512,256]{1,0:T(8,128)(2,1)}, bf16[512,256]{1,0:T(8,128)(2,1)S(1)}, u32[]{:S(2)}, u32[]{:S(2)}) %collective-permute-start.8) | collective-permute-done | bytes 262176 | tf_op jit(solution)/shard_map/ppermute | solution.py:143
  55.8 1.0 constant_dynamic-update-slice_fusion.9
  56.8 1.3 copy-done
  58.2 37.5 %shard_map.103 = (f32[32,144,128]{2,1,0:T(8,128)}, f32[16,64,256]{2,1,0:T(8,128)}) custom-call(s32[7,14]{1,0:T(8,128)} %stack.36.tab, bf16[14,64,4096]{2,1,0:T(8,128)(2,1)} %values_ref.1, bf16[64,64,256]{2,1,0:T(8,128)(2,1)} %bitcast.62, bf16[16,64,256]{2,1,0:T(8,128)(2,1)} %bitcast.63, bf16[64,64,256]{2,1,0:T(8,128)(2,1)} %bitcast.64), custom_call_target="tpu_custom_call" | custom-call | tf_op jit(solution)/shard_map/pallas_call | solution.py:123
  95.6 2.8 %convert_element_type.19 = f16[32,144,128]{2,1,0:T(8,128)(2,1)} convert(f32[32,144,128]{2,1,0:T(8,128)} %get-tuple-element.7) | non-fusion elementwise | flops 589824 | bytes 3538944 | tf_op jit(solution)/shard_map/convert_element_type | solution.py:163
  98.5 10.6 %all-to-all-start = ((f16[32,144,128]{2,1,0:T(8,128)(2,1)}), f16[32,144,128]{2,1,0:T(8,128)(2,1)S(1)}, u32[]{:S(2)}, u32[]{:S(2)}) async-start(f16[32,144,128]{2,1,0:T(8,128)(2,1)} %convert_element_type.19), calls=%async_computation | async-start | bytes 2359296 | tf_op jit(solution)/shard_map/all_to_all | solution.py:164
  109.6 2.0 %collective-permute-start.13 = (f32[128,256]{1,0:T(8,128)S(1)}, f32[128,256]{1,0:T(8,128)S(1)}, u32[]{:S(2)}, u32[]{:S(2)}) collective-permute-start(f32[128,256]{1,0:T(8,128)S(1)} %get-tuple-element.24), channel_id=1, source_target_pairs={{0,96},{32,128},{64,160},{96,192},{128,224},{160,0},{192,32},{224,... | collective-permute-start | bytes 393224 | tf_op jit(solution)/shard_map/ppermute | solution.py:143
  111.6 1.5 %collective-permute-start.14 = (f32[128,256]{1,0:T(8,128)S(1)}, f32[128,256]{1,0:T(8,128)S(1)}, u32[]{:S(2)}, u32[]{:S(2)}) collective-permute-start(f32[128,256]{1,0:T(8,128)S(1)} %get-tuple-element.23), channel_id=1, source_target_pairs={{0,128},{32,160},{64,192},{96,224},{128,0},{160,32},{192,64},{224,... | collective-permute-start | bytes 393224 | tf_op jit(solution)/shard_map/ppermute | solution.py:143
  113.2 1.5 collective-permute-start.15
  114.7 1.3 collective-permute-start.16
  115.9 3.0 %collective-permute-start.17 = (f32[128,256]{1,0:T(8,128)S(1)}, f32[128,256]{1,0:T(8,128)}, u32[]{:S(2)}, u32[]{:S(2)}) collective-permute-start(f32[128,256]{1,0:T(8,128)S(1)} %get-tuple-element.20), channel_id=1, source_target_pairs={{0,224},{32,0},{64,32},{96,64},{128,96},{160,128},{192,160},{224,1... | collective-permute-start | bytes 393224 | tf_op jit(solution)/shard_map/ppermute | solution.py:143
  119.5 3.4 %collective-permute-done.15 = f32[128,256]{1,0:T(8,128)} collective-permute-done((f32[128,256]{1,0:T(8,128)S(1)}, f32[128,256]{1,0:T(8,128)}, u32[]{:S(2)}, u32[]{:S(2)}) %collective-permute-start.15) | collective-permute-done | bytes 131104 | tf_op jit(solution)/shard_map/ppermute | solution.py:143
  123.4 1.8 %fusion.10 = f32[128,256]{1,0:T(8,128)} fusion(f32[128,256]{1,0:T(8,128)} %collective-permute-done.17, f32[128,256]{1,0:T(8,128)} %collective-permute-done.16, f32[128,256]{1,0:T(8,128)} %collective-permute-done.15, f32[128,256]{1,0:T(8,128)S(1)} %collective-permute-done.14, f32[128,256]{1,0:T(8,128)S(1)} %collective-permute-done.13, ...), kind=kLoop, calls=%fused_computation.15 | loop fusion | flops 327680 | bytes 1245188 | tf_op jit(solution)/shard_map/sub | solution.py:184
  125.2 14.1 %all-to-all-done = f16[32,144,128]{2,1,0:T(8,128)(2,1)S(1)} async-done(((f16[32,144,128]{2,1,0:T(8,128)(2,1)}), f16[32,144,128]{2,1,0:T(8,128)(2,1)S(1)}, u32[]{:S(2)}, u32[]{:S(2)}) %all-to-all-start) | async-done | bytes 1179680 | tf_op jit(solution)/shard_map/all_to_all | solution.py:164
  141.4 0.7 broadcast_in_dim.27
  142.0 4.3 %all-to-all-start.1 = ((f32[8,8,128]{2,1,0:T(8,128)}), f32[8,8,128]{2,1,0:T(8,128)S(1)}, u32[]{:S(2)}, u32[]{:S(2)}) async-start(f32[8,8,128]{2,1,0:T(8,128)} %broadcast_in_dim.27), calls=%async_computation.1 | async-start | bytes 65536 | tf_op jit(solution)/shard_map/all_to_all | solution.py:181
  146.9 0.7 bitcast_subtract_fusion
  147.6 2.7 %all-to-all-done.1 = f32[8,8,128]{2,1,0:T(8,128)S(1)} async-done(((f32[8,8,128]{2,1,0:T(8,128)}), f32[8,8,128]{2,1,0:T(8,128)S(1)}, u32[]{:S(2)}, u32[]{:S(2)}) %all-to-all-start.1) | async-done | bytes 32800 | tf_op jit(solution)/shard_map/all_to_all | solution.py:181
  (63 shorter events, 13.2 us)
Async XLA Ops:
  0.6 49.1 %copy-start.4 = (s32[14]{0:T(128)S(1)}, s32[14]{0:T(128)}, u32[]{:S(2)}) copy-start(s32[14]{0:T(128)} %param.9) | copy-start | bytes 172
  0.6 49.1 %copy-start.7 = (s32[14]{0:T(128)S(1)}, s32[14]{0:T(128)}, u32[]{:S(2)}) copy-start(s32[14]{0:T(128)} %param.12) | copy-start | bytes 172
  0.7 50.4 %copy-start.5 = (s32[14]{0:T(128)S(1)}, s32[14]{0:T(128)}, u32[]{:S(2)}) copy-start(s32[14]{0:T(128)} %param.10) | copy-start | bytes 172
  0.7 50.4 %copy-start.6 = (s32[14]{0:T(128)S(1)}, s32[14]{0:T(128)}, u32[]{:S(2)}) copy-start(s32[14]{0:T(128)} %param.11) | copy-start | bytes 172
  0.7 16.3 %collective-permute-start = (bf16[128,256]{1,0:T(8,128)(2,1)}, bf16[128,256]{1,0:T(8,128)(2,1)S(1)}, u32[]{:S(2)}, u32[]{:S(2)}) collective-permute-start(bf16[128,256]{1,0:T(8,128)(2,1)} %param.13), channel_id=1, source_target_pairs={{0,4},{4,8},{8,12},{12,16},{16,20},{20,24},{24,28},{28,0},{1,5},{5... | collective-permute-start | bytes 196616 | tf_op jit(solution)/shard_map/ppermute | solution.py:143
  2.7 17.6 %collective-permute-start.1 = (bf16[128,256]{1,0:T(8,128)(2,1)}, bf16[128,256]{1,0:T(8,128)(2,1)S(1)}, u32[]{:S(2)}, u32[]{:S(2)}) collective-permute-start(bf16[128,256]{1,0:T(8,128)(2,1)} %param.13), channel_id=1, source_target_pairs={{0,8},{4,12},{8,16},{12,20},{16,24},{20,28},{24,0},{28,4},{1,9},{5... | collective-permute-start | bytes 196616 | tf_op jit(solution)/shard_map/ppermute | solution.py:143
  5.9 16.0 %collective-permute-start.2 = (bf16[128,256]{1,0:T(8,128)(2,1)}, bf16[128,256]{1,0:T(8,128)(2,1)S(1)}, u32[]{:S(2)}, u32[]{:S(2)}) collective-permute-start(bf16[128,256]{1,0:T(8,128)(2,1)} %param.13), channel_id=1, source_target_pairs={{0,12},{4,16},{8,20},{12,24},{16,28},{20,0},{24,4},{28,8},{1,13},{... | collective-permute-start | bytes 196616 | tf_op jit(solution)/shard_map/ppermute | solution.py:143
  10.0 12.6 %collective-permute-start.3 = (bf16[128,256]{1,0:T(8,128)(2,1)}, bf16[128,256]{1,0:T(8,128)(2,1)S(1)}, u32[]{:S(2)}, u32[]{:S(2)}) collective-permute-start(bf16[128,256]{1,0:T(8,128)(2,1)} %param.13), channel_id=1, source_target_pairs={{0,16},{4,20},{8,24},{12,28},{16,0},{20,4},{24,8},{28,12},{1,17},{... | collective-permute-start | bytes 196616 | tf_op jit(solution)/shard_map/ppermute | solution.py:143
  10.5 12.7 %collective-permute-start.4 = (bf16[128,256]{1,0:T(8,128)(2,1)}, bf16[128,256]{1,0:T(8,128)(2,1)S(1)}, u32[]{:S(2)}, u32[]{:S(2)}) collective-permute-start(bf16[128,256]{1,0:T(8,128)(2,1)} %param.13), channel_id=1, source_target_pairs={{0,20},{4,24},{8,28},{12,0},{16,4},{20,8},{24,12},{28,16},{1,21},{... | collective-permute-start | bytes 196616 | tf_op jit(solution)/shard_map/ppermute | solution.py:143
  17.0 7.8 %collective-permute-start.5 = (bf16[128,256]{1,0:T(8,128)(2,1)}, bf16[128,256]{1,0:T(8,128)(2,1)S(1)}, u32[]{:S(2)}, u32[]{:S(2)}) collective-permute-start(bf16[128,256]{1,0:T(8,128)(2,1)} %param.13), channel_id=1, source_target_pairs={{0,24},{4,28},{8,0},{12,4},{16,8},{20,12},{24,16},{28,20},{1,25},{... | collective-permute-start | bytes 196616 | tf_op jit(solution)/shard_map/ppermute | solution.py:143
  20.3 5.6 %collective-permute-start.6 = (bf16[128,256]{1,0:T(8,128)(2,1)}, bf16[128,256]{1,0:T(8,128)(2,1)S(1)}, u32[]{:S(2)}, u32[]{:S(2)}) collective-permute-start(bf16[128,256]{1,0:T(8,128)(2,1)} %param.13), channel_id=1, source_target_pairs={{0,28},{4,0},{8,4},{12,8},{16,12},{20,16},{24,20},{28,24},{1,29},{... | collective-permute-start | bytes 196616 | tf_op jit(solution)/shard_map/ppermute | solution.py:143
  26.5 18.5 %collective-permute-start.7 = (bf16[1024,256]{1,0:T(8,128)(2,1)}, bf16[1024,256]{1,0:T(8,128)(2,1)S(1)}, u32[]{:S(2)}, u32[]{:S(2)}) collective-permute-start(bf16[1024,256]{1,0:T(8,128)(2,1)} %get-tuple-element.26), channel_id=1, source_target_pairs={{0,1},{1,2},{2,3},{3,0},{4,5},{5,6},{6,7},{7,4},{8,9},{9,10},{10,1... | collective-permute-start | bytes 1572872 | tf_op jit(solution)/shard_map/ppermute | solution.py:143
  28.0 18.0 %collective-permute-start.9 = (bf16[1024,256]{1,0:T(8,128)(2,1)}, bf16[1024,256]{1,0:T(8,128)(2,1)S(1)}, u32[]{:S(2)}, u32[]{:S(2)}) collective-permute-start(bf16[1024,256]{1,0:T(8,128)(2,1)} %get-tuple-element.26), channel_id=1, source_target_pairs={{0,3},{1,0},{2,1},{3,2},{4,7},{5,4},{6,5},{7,6},{8,11},{9,8},{10,9... | collective-permute-start | bytes 1572872 | tf_op jit(solution)/shard_map/ppermute | solution.py:143
  45.7 10.0 %collective-permute-start.8 = (bf16[512,256]{1,0:T(8,128)(2,1)}, bf16[512,256]{1,0:T(8,128)(2,1)S(1)}, u32[]{:S(2)}, u32[]{:S(2)}) collective-permute-start(bf16[512,256]{1,0:T(8,128)(2,1)} %slice.62), channel_id=1, source_target_pairs={{0,1},{1,2},{2,3},{3,0},{4,5},{5,6},{6,7},{7,4},{8,9},{9,10},{10,1... | collective-permute-start | bytes 786440 | tf_op jit(solution)/shard_map/ppermute | solution.py:143
  46.8 9.1 %collective-permute-start.10 = (bf16[512,256]{1,0:T(8,128)(2,1)}, bf16[512,256]{1,0:T(8,128)(2,1)}, u32[]{:S(2)}, u32[]{:S(2)}) collective-permute-start(bf16[512,256]{1,0:T(8,128)(2,1)} %slice.63), channel_id=1, source_target_pairs={{0,3},{1,0},{2,1},{3,2},{4,7},{5,4},{6,5},{7,6},{8,11},{9,8},{10,9... | collective-permute-start | bytes 786440 | tf_op jit(solution)/shard_map/ppermute | solution.py:143
  56.8 1.3 copy-start
  98.5 10.7 %copy-start.1 = (f32[16,64,256]{2,1,0:T(8,128)S(1)}, f32[16,64,256]{2,1,0:T(8,128)}, u32[]{:S(2)}) copy-start(f32[16,64,256]{2,1,0:T(8,128)} %get-tuple-element.10) | copy-start | bytes 3145732
  98.5 25.0 %copy-start.2 = (bf16[128,256]{1,0:T(8,128)(2,1)S(1)}, bf16[128,256]{1,0:T(8,128)(2,1)}, u32[]{:S(2)}) copy-start(bf16[128,256]{1,0:T(8,128)(2,1)} %param.14) | copy-start | bytes 196612
  98.5 40.8 %all-to-all-start = ((f16[32,144,128]{2,1,0:T(8,128)(2,1)}), f16[32,144,128]{2,1,0:T(8,128)(2,1)S(1)}, u32[]{:S(2)}, u32[]{:S(2)}) async-start(f16[32,144,128]{2,1,0:T(8,128)(2,1)} %convert_element_type.19), calls=%async_computation | async-start | bytes 2359296 | tf_op jit(solution)/shard_map/all_to_all | solution.py:164
  109.3 37.6 %copy-start.3 = (bf16[128,256]{1,0:T(8,128)(2,1)S(1)}, bf16[128,256]{1,0:T(8,128)(2,1)}, u32[]{:S(2)}) copy-start(bf16[128,256]{1,0:T(8,128)(2,1)} %param.13) | copy-start | bytes 196612
  109.3 5.4 %collective-permute-start.11 = (f32[128,256]{1,0:T(8,128)S(1)}, f32[128,256]{1,0:T(8,128)S(1)}, u32[]{:S(2)}, u32[]{:S(2)}) collective-permute-start(f32[128,256]{1,0:T(8,128)S(1)} %get-tuple-element.19), channel_id=1, source_target_pairs={{0,32},{32,64},{64,96},{96,128},{128,160},{160,192},{192,224},{224... | collective-permute-start | bytes 393224 | tf_op jit(solution)/shard_map/ppermute | solution.py:143
  109.3 6.6 %collective-permute-start.12 = (f32[128,256]{1,0:T(8,128)S(1)}, f32[128,256]{1,0:T(8,128)S(1)}, u32[]{:S(2)}, u32[]{:S(2)}) collective-permute-start(f32[128,256]{1,0:T(8,128)S(1)} %get-tuple-element.25), channel_id=1, source_target_pairs={{0,64},{32,96},{64,128},{96,160},{128,192},{160,224},{192,0},{224,... | collective-permute-start | bytes 393224 | tf_op jit(solution)/shard_map/ppermute | solution.py:143
  109.6 9.4 %collective-permute-start.13 = (f32[128,256]{1,0:T(8,128)S(1)}, f32[128,256]{1,0:T(8,128)S(1)}, u32[]{:S(2)}, u32[]{:S(2)}) collective-permute-start(f32[128,256]{1,0:T(8,128)S(1)} %get-tuple-element.24), channel_id=1, source_target_pairs={{0,96},{32,128},{64,160},{96,192},{128,224},{160,0},{192,32},{224,... | collective-permute-start | bytes 393224 | tf_op jit(solution)/shard_map/ppermute | solution.py:143
  111.6 7.9 %collective-permute-start.14 = (f32[128,256]{1,0:T(8,128)S(1)}, f32[128,256]{1,0:T(8,128)S(1)}, u32[]{:S(2)}, u32[]{:S(2)}) collective-permute-start(f32[128,256]{1,0:T(8,128)S(1)} %get-tuple-element.23), channel_id=1, source_target_pairs={{0,128},{32,160},{64,192},{96,224},{128,0},{160,32},{192,64},{224,... | collective-permute-start | bytes 393224 | tf_op jit(solution)/shard_map/ppermute | solution.py:143
  113.2 9.7 %collective-permute-start.15 = (f32[128,256]{1,0:T(8,128)S(1)}, f32[128,256]{1,0:T(8,128)}, u32[]{:S(2)}, u32[]{:S(2)}) collective-permute-start(f32[128,256]{1,0:T(8,128)S(1)} %get-tuple-element.22), channel_id=1, source_target_pairs={{0,160},{32,192},{64,224},{96,0},{128,32},{160,64},{192,96},{224,1... | collective-permute-start | bytes 393224 | tf_op jit(solution)/shard_map/ppermute | solution.py:143
  114.7 8.5 %collective-permute-start.16 = (f32[128,256]{1,0:T(8,128)S(1)}, f32[128,256]{1,0:T(8,128)}, u32[]{:S(2)}, u32[]{:S(2)}) collective-permute-start(f32[128,256]{1,0:T(8,128)S(1)} %get-tuple-element.21), channel_id=1, source_target_pairs={{0,192},{32,224},{64,0},{96,32},{128,64},{160,96},{192,128},{224,1... | collective-permute-start | bytes 393224 | tf_op jit(solution)/shard_map/ppermute | solution.py:143
  115.9 7.5 %collective-permute-start.17 = (f32[128,256]{1,0:T(8,128)S(1)}, f32[128,256]{1,0:T(8,128)}, u32[]{:S(2)}, u32[]{:S(2)}) collective-permute-start(f32[128,256]{1,0:T(8,128)S(1)} %get-tuple-element.20), channel_id=1, source_target_pairs={{0,224},{32,0},{64,32},{96,64},{128,96},{160,128},{192,160},{224,1... | collective-permute-start | bytes 393224 | tf_op jit(solution)/shard_map/ppermute | solution.py:143
  142.0 8.3 %all-to-all-start.1 = ((f32[8,8,128]{2,1,0:T(8,128)}), f32[8,8,128]{2,1,0:T(8,128)S(1)}, u32[]{:S(2)}, u32[]{:S(2)}) async-start(f32[8,8,128]{2,1,0:T(8,128)} %broadcast_in_dim.27), calls=%async_computation.1 | async-start | bytes 65536 | tf_op jit(solution)/shard_map/all_to_all | solution.py:181
